TPU v7x, 256 devices: a whole 4x4x8 slice. The times are simulated.
256 devices in a mesh: dp: 32 (over z, y), tensor: 8 (over x, core).
Axes of the slice: x: 4, y: 4, z: 8, core: 2. Of those that a mesh axis runs over, the one named last changes fastest.
Arguments:
- attention: bfloat16 [16384, 4096], P('dp', 'tensor'), may hold values from -0.44921875 to 0.546875
- cotangent: bfloat16 [16384, 2048], P('dp', 'tensor'), may hold values from -0.5 to 1.5
- projection: bfloat16 [4096, 2048], P(None, 'tensor'), may hold values from -0.125 to 0.125
Outputs:
- input_grad: bfloat16 [16384, 4096], P('dp', 'tensor')
- combined: float32 [4096, 2048], P(None, 'tensor')
All inputs are finite; a program needn't handle non-finite values.
Results may differ from a plain program's by a relative error of at most 0.0004.
Values may be sent and summed in bfloat16 or wider, within the bound.
A program may use at most 64 MiB of HBM per device.

v0:
```python
import jax
import jax.numpy as jnp
from jax import lax
from jax.sharding import Mesh
from jax.sharding import PartitionSpec as P

DP = ("dp_0", "dp_1")


epsilon = 1e-06


def from_everyone(shard, axis):
    copies = jnp.broadcast_to(shard, (lax.axis_size(axis), *shard.shape))
    return lax.all_to_all(copies, axis, split_axis=0, concat_axis=0, tiled=True)


def of_everyone(shard, axis):
    everything = from_everyone(shard, axis)
    return jnp.sum(everything, axis=0)


def swapped(value, axis, stride):
    mask = 2**stride
    pairs = [(source, source ^ mask) for source in range(lax.axis_size(axis))]
    return lax.ppermute(value, axis, pairs)


def gather_axes(shard, axes, dim):
    if not axes:
        return shard
    nearer = lax.all_gather(shard, axes[-1], axis=dim, tiled=True)
    return gather_axes(nearer, axes[:-1], dim)


def level_totals(local_dots, depth):
    totals = of_everyone(local_dots, "tensor")
    for shift_bit in range(depth + 1):
        totals = totals + swapped(totals, DP, shift_bit)
    return totals


def halving_merge(block):
    replica_count = lax.axis_size(DP)
    levels = replica_count.bit_length() - 1
    replica = lax.axis_index(DP)
    portion = block
    for depth in range(levels):
        halfway = portion.shape[0] // 2
        upper_bit = jnp.right_shift(replica, depth) & 1
        retained = lax.dynamic_slice_in_dim(portion, upper_bit * halfway, halfway, 0)
        outgoing = lax.dynamic_slice_in_dim(portion, (1 - upper_bit) * halfway, halfway, 0)
        incoming = swapped(outgoing, DP, depth)
        is_lower = upper_bit == 0
        lower_vec = jnp.where(is_lower, retained, incoming)
        upper_vec = jnp.where(is_lower, incoming, retained)
        local_dots = jnp.stack(
            [
                jnp.sum(lower_vec * lower_vec),
                jnp.sum(upper_vec * upper_vec),
                jnp.sum(lower_vec * upper_vec),
            ]
        )
        totals = level_totals(local_dots, depth)
        lower_sq = totals[0] + epsilon
        upper_sq = totals[1] + epsilon
        cross = totals[2]
        portion = (1.0 - cross / (2.0 * lower_sq)) * lower_vec + (
            1.0 - cross / (2.0 * upper_sq)
        ) * upper_vec
    return (portion, levels)


def on_device(attention, cotangent, projection):
    term = lax.dot_general(
        cotangent, projection, (((1,), (1,)), ((), ())), preferred_element_type=jnp.float32
    )
    input_grad = lax.psum_scatter(term, "tensor", scatter_dimension=1, tiled=True).astype(
        jnp.bfloat16
    )
    grad_block = lax.dot_general(
        lax.all_gather(attention, "tensor", axis=1, tiled=True),
        cotangent,
        (((0,), (0,)), ((), ())),
        preferred_element_type=jnp.float32,
    )
    merged, levels = halving_merge(grad_block)
    gathered = gather_axes(merged, DP, 0)
    col_width = merged.shape[1]
    shaped = gathered.reshape((2,) * levels + (merged.shape[0], col_width))
    order = tuple(range(levels - 1, -1, -1)) + (levels, levels + 1)
    combined = jnp.transpose(shaped, order).reshape(-1, col_width)
    return (input_grad, combined)


def solution(mesh):
    finer = Mesh(mesh.devices.reshape(8, 4, mesh.shape["tensor"]), ("dp_0", "dp_1", "tensor"))
    return jax.shard_map(
        on_device,
        mesh=finer,
        in_specs=(P(DP, "tensor"), P(DP, "tensor"), P(None, "tensor")),
        out_specs=(P(DP, "tensor"), P(None, "tensor")),
        check_vma=False,
    )
```

profile of v0, /device:TPU:2, one launch (start us, length us, event | category | flops | bytes accessed | tf_op | source)
XLA Modules:
  0.0 393.8 jit_solution(1220312620704826279)
XLA Ops:
  8.8 5.5 %fusion.5 = f32[512,4096]{1,0:T(8,128)} fusion(bf16[512,256]{1,0:T(8,128)(2,1)} %param.4, bf16[4096,256]{1,0:T(8,128)(2,1)S(1)} %copy-done), kind=kOutput, calls=%fused_computation.45 | convolution fusion | flops 1073741824 | bytes 10747904 | tf_op jit(solution)/shard_map/dot_general | solution.py:75
  14.3 32.2 %all-gather.3.cloned.1.call-done = bf16[512,4096]{1,0:T(8,128)(2,1)} async-done(((bf16[512,512]{1,0:T(8,128)(2,1)}), bf16[512,4096]{1,0:T(8,128)(2,1)}) %all-gather.3.cloned.1.call-update) | async-done | bytes 4194320 | tf_op jit(solution)/shard_map/all_gather | solution.py:82
  46.5 3.5 fusion.6
  54.1 46.6 %collective-permute-done = f32[2048,256]{1,0:T(8,128)} collective-permute-done((f32[2048,256]{1,0:T(8,128)}, f32[2048,256]{1,0:T(8,128)}, u32[]{:S(2)}, u32[]{:S(2)}) %collective-permute-start) | collective-permute-done | bytes 2097184 | tf_op jit(solution)/shard_map/ppermute | solution.py:26
  100.7 5.5 %multiply_reduce_fusion.2 = (f32[]{:T(128)}, f32[]{:T(128)}, f32[]{:T(128)}, f32[2048,256]{1,0:T(8,128)}, f32[2048,256]{1,0:T(8,128)}) fusion(f32[2048,256]{1,0:T(8,128)} %collective-permute-done, f32[4096,256]{1,0:T(8,128)} %copy-done.1, s32[]{:T(128)S(6)} %select_n.95, pred[]{:T(512)S(6)} %eq.19), kind=kLoop, calls=%fused_computation.3 | loop fusion | flops 4194301 | bytes 8388625 | tf_op jit(solution)/shard_map/reduce_sum | solution.py:59
  108.8 4.8 %all-to-all-start = ((f32[8,1,3]{2,1,0:T(1,128)}), f32[8,1,3]{2,1,0:T(1,128)S(1)}, u32[]{:S(2)}, u32[]{:S(2)}) async-start(f32[8,1,3]{2,1,0:T(1,128)} %broadcast_in_dim.15), calls=%async_computation.1 | async-start | bytes 8192 | tf_op jit(solution)/shard_map/all_to_all | solution.py:15
  113.6 3.8 all-to-all-done
  128.0 3.1 collective-permute-start.2
  131.1 22.3 %collective-permute-done.2 = f32[1024,256]{1,0:T(8,128)} collective-permute-done((f32[1024,256]{1,0:T(8,128)S(1)}, f32[1024,256]{1,0:T(8,128)}, u32[]{:S(2)}, u32[]{:S(2)}) %collective-permute-start.2) | collective-permute-done | bytes 1048608 | tf_op jit(solution)/shard_map/ppermute | solution.py:26
  153.4 3.5 multiply_reduce_fusion.5
  159.5 4.7 %all-to-all-start.1 = ((f32[8,1,3]{2,1,0:T(1,128)}), f32[8,1,3]{2,1,0:T(1,128)S(1)}, u32[]{:S(2)}, u32[]{:S(2)}) async-start(f32[8,1,3]{2,1,0:T(1,128)} %broadcast_in_dim.16), calls=%async_computation.2 | async-start | bytes 8192 | tf_op jit(solution)/shard_map/all_to_all | solution.py:15
  164.2 3.8 all-to-all-done.1
  171.6 3.0 collective-permute-start.4
  183.9 9.9 %collective-permute-done.5 = f32[512,256]{1,0:T(8,128)} collective-permute-done((f32[512,256]{1,0:T(8,128)S(1)}, f32[512,256]{1,0:T(8,128)}, u32[]{:S(2)}, u32[]{:S(2)}) %collective-permute-start.5) | collective-permute-done | bytes 524320 | tf_op jit(solution)/shard_map/ppermute | solution.py:26
  193.8 2.8 multiply_reduce_fusion.8
  199.0 4.7 %all-to-all-start.2 = ((f32[8,1,3]{2,1,0:T(1,128)}), f32[8,1,3]{2,1,0:T(1,128)S(1)}, u32[]{:S(2)}, u32[]{:S(2)}) async-start(f32[8,1,3]{2,1,0:T(1,128)} %broadcast_in_dim.17), calls=%async_computation.3 | async-start | bytes 8192 | tf_op jit(solution)/shard_map/all_to_all | solution.py:15
  203.7 3.8 all-to-all-done.2
  211.1 3.0 collective-permute-start.7
  226.5 8.5 %collective-permute-done.9 = f32[256,256]{1,0:T(8,128)S(1)} collective-permute-done((f32[256,256]{1,0:T(8,128)S(1)}, f32[256,256]{1,0:T(8,128)S(1)}, u32[]{:S(2)}, u32[]{:S(2)}) %collective-permute-start.9) | collective-permute-done | bytes 262176 | tf_op jit(solution)/shard_map/ppermute | solution.py:26
  238.3 4.7 %all-to-all-start.3 = ((f32[8,1,3]{2,1,0:T(1,128)}), f32[8,1,3]{2,1,0:T(1,128)S(1)}, u32[]{:S(2)}, u32[]{:S(2)}) async-start(f32[8,1,3]{2,1,0:T(1,128)} %broadcast_in_dim.18), calls=%async_computation.4 | async-start | bytes 8192 | tf_op jit(solution)/shard_map/all_to_all | solution.py:15
  243.0 3.8 all-to-all-done.3
  250.6 3.0 collective-permute-start.11
  256.2 2.9 collective-permute-done.12
  266.7 5.8 %collective-permute-start.14 = (f32[128,256]{1,0:T(8,128)S(1)}, f32[128,256]{1,0:T(8,128)S(1)}, u32[]{:S(2)}, u32[]{:S(2)}) collective-permute-start(f32[128,256]{1,0:T(8,128)S(1)} %constant_dynamic-slice_fusion), channel_id=1, source_target_pairs={{0,128},{8,136},{16,144},{24,152},{32,160},{40,168},{48,176},{56,1... | collective-permute-start | bytes 393224 | tf_op jit(solution)/shard_map/ppermute | solution.py:26
  272.5 3.2 collective-permute-done.14
  278.4 7.6 %all_to_all.30 = f32[8,1,3]{2,1,0:T(1,128)S(1)} all-to-all(f32[8,1,3]{2,1,0:T(1,128)S(1)} %broadcast_in_dim.19), channel_id=1, replica_groups=mesh['dp_0'=8,'dp_1'=4,'tensor'=8] {'tensor'}, dimensions={0} | all-to-all | bytes 192 | tf_op jit(solution)/shard_map/all_to_all | solution.py:15
  289.6 3.0 collective-permute-start.16
  298.2 3.4 collective-permute-start.18
  303.1 6.1 %collective-permute-start.19 = (f32[3]{0:T(128)S(1)}, f32[3]{0:T(128)S(1)}, u32[]{:S(2)}, u32[]{:S(2)}) collective-permute-start(f32[3]{0:T(128)S(1)} %add.171), channel_id=1, source_target_pairs={{0,128},{8,136},{16,144},{24,152},{32,160},{40,168},{48,176},{56,1... | collective-permute-start | bytes 44 | tf_op jit(solution)/shard_map/ppermute | solution.py:26
  313.8 13.9 %all_gather.10 = f32[512,256]{1,0:T(8,128)} all-gather(f32[128,256]{1,0:T(8,128)S(1)} %multiply_add_fusion.4), channel_id=1, replica_groups=mesh['dp_0'=8,'dp_1'=4,'tensor'=8] {'dp_1'}, dimensions={0}, use_global_device_ids=true | all-gather | bytes 655360 | tf_op jit(solution)/shard_map/all_gather | solution.py:32
  329.8 52.8 %all-gather.5.cloned.1.call-done = f32[4096,256]{1,0:T(8,128)} async-done(((f32[512,256]{1,0:T(8,128)}), f32[4096,256]{1,0:T(8,128)}) %all-gather.5.cloned.1.call-update) | async-done | bytes 4194320 | tf_op jit(solution)/shard_map/all_gather | solution.py:32
  382.6 4.7 %copy.18 = f32[2,2,2,2,2,128,256]{6,5,4,3,2,1,0:T(8,128)} copy(f32[2,2,2,2,2,128,256]{6,5,0,1,2,3,4:T(8,128)} %bitcast.33) | data formatting | bytes 8388608 | tf_op jit(solution)/shard_map/transpose | solution.py:92
  (91 shorter events, 77.8 us)
Async XLA Ops:
  7.2 1.6 copy-start
  7.2 39.3 %all-gather.3.cloned.1.call-start = ((), (), s32[]{:S(2)}) async-start(), calls=%async_computation.7 | async-start | bytes 4718592 | tf_op jit(solution)/shard_map/all_gather | solution.py:82
  7.9 319.8 %reduce-scatter.2.cloned.1.call-start = ((), (), s32[]{:S(2)}) async-start(), calls=%async_computation.6 | async-start | bytes 9437184 | tf_op jit(solution)/shard_map/reduce_scatter | solution.py:78
  14.2 32.3 %copy-start.4 = (bf16[512,256]{1,0:T(8,128)(2,1)S(1)}, bf16[512,256]{1,0:T(8,128)(2,1)}, u32[]{:S(2)}) copy-start(bf16[512,256]{1,0:T(8,128)(2,1)} %param.4) | copy-start | bytes 786436
  50.0 2.6 copy-start.1
  52.6 48.1 %collective-permute-start = (f32[2048,256]{1,0:T(8,128)}, f32[2048,256]{1,0:T(8,128)}, u32[]{:S(2)}, u32[]{:S(2)}) collective-permute-start(f32[2048,256]{1,0:T(8,128)} %constant_dynamic-slice_fusion.4), channel_id=1, source_target_pairs={{0,8},{8,0},{16,24},{24,16},{32,40},{40,32},{48,56},{56,48},{64,72... | collective-permute-start | bytes 6291464 | tf_op jit(solution)/shard_map/ppermute | solution.py:26
  108.8 8.6 %all-to-all-start = ((f32[8,1,3]{2,1,0:T(1,128)}), f32[8,1,3]{2,1,0:T(1,128)S(1)}, u32[]{:S(2)}, u32[]{:S(2)}) async-start(f32[8,1,3]{2,1,0:T(1,128)} %broadcast_in_dim.15), calls=%async_computation.1 | async-start | bytes 8192 | tf_op jit(solution)/shard_map/all_to_all | solution.py:15
  117.4 3.6 collective-permute-start.1
  126.6 1.3 copy-start.2
  128.0 25.4 %collective-permute-start.2 = (f32[1024,256]{1,0:T(8,128)S(1)}, f32[1024,256]{1,0:T(8,128)}, u32[]{:S(2)}, u32[]{:S(2)}) collective-permute-start(f32[1024,256]{1,0:T(8,128)S(1)} %constant_dynamic-slice_fusion.3), channel_id=1, source_target_pairs={{0,16},{8,24},{16,0},{24,8},{32,48},{40,56},{48,32},{56,40},{64,80... | collective-permute-start | bytes 3145736 | tf_op jit(solution)/shard_map/ppermute | solution.py:26
  159.5 8.4 %all-to-all-start.1 = ((f32[8,1,3]{2,1,0:T(1,128)}), f32[8,1,3]{2,1,0:T(1,128)S(1)}, u32[]{:S(2)}, u32[]{:S(2)}) async-start(f32[8,1,3]{2,1,0:T(1,128)} %broadcast_in_dim.16), calls=%async_computation.2 | async-start | bytes 8192 | tf_op jit(solution)/shard_map/all_to_all | solution.py:15
  168.0 3.6 collective-permute-start.3
  171.6 5.0 %collective-permute-start.4 = (f32[3]{0:T(128)S(1)}, f32[3]{0:T(128)S(1)}, u32[]{:S(2)}, u32[]{:S(2)}) collective-permute-start(f32[3]{0:T(128)S(1)} %add.144), channel_id=1, source_target_pairs={{0,16},{8,24},{16,0},{24,8},{32,48},{40,56},{48,32},{56,40},{64,80... | collective-permute-start | bytes 44 | tf_op jit(solution)/shard_map/ppermute | solution.py:26
  181.2 1.0 copy-start.3
  182.2 11.5 %collective-permute-start.5 = (f32[512,256]{1,0:T(8,128)S(1)}, f32[512,256]{1,0:T(8,128)}, u32[]{:S(2)}, u32[]{:S(2)}) collective-permute-start(f32[512,256]{1,0:T(8,128)S(1)} %constant_dynamic-slice_fusion.2), channel_id=1, source_target_pairs={{0,32},{8,40},{16,48},{24,56},{32,0},{40,8},{48,16},{56,24},{64,96... | collective-permute-start | bytes 1572872 | tf_op jit(solution)/shard_map/ppermute | solution.py:26
  199.0 8.4 %all-to-all-start.2 = ((f32[8,1,3]{2,1,0:T(1,128)}), f32[8,1,3]{2,1,0:T(1,128)S(1)}, u32[]{:S(2)}, u32[]{:S(2)}) async-start(f32[8,1,3]{2,1,0:T(1,128)} %broadcast_in_dim.17), calls=%async_computation.3 | async-start | bytes 8192 | tf_op jit(solution)/shard_map/all_to_all | solution.py:15
  207.5 3.6 collective-permute-start.6
  211.1 5.0 %collective-permute-start.7 = (f32[3]{0:T(128)S(1)}, f32[3]{0:T(128)S(1)}, u32[]{:S(2)}, u32[]{:S(2)}) collective-permute-start(f32[3]{0:T(128)S(1)} %add.151), channel_id=1, source_target_pairs={{0,16},{8,24},{16,0},{24,8},{32,48},{40,56},{48,32},{56,40},{64,80... | collective-permute-start | bytes 44 | tf_op jit(solution)/shard_map/ppermute | solution.py:26
  216.2 3.5 collective-permute-start.8
  223.9 11.2 %collective-permute-start.9 = (f32[256,256]{1,0:T(8,128)S(1)}, f32[256,256]{1,0:T(8,128)S(1)}, u32[]{:S(2)}, u32[]{:S(2)}) collective-permute-start(f32[256,256]{1,0:T(8,128)S(1)} %constant_dynamic-slice_fusion.1), channel_id=1, source_target_pairs={{0,64},{8,72},{16,80},{24,88},{32,96},{40,104},{48,112},{56,120},{... | collective-permute-start | bytes 786440 | tf_op jit(solution)/shard_map/ppermute | solution.py:26
  238.3 8.4 %all-to-all-start.3 = ((f32[8,1,3]{2,1,0:T(1,128)}), f32[8,1,3]{2,1,0:T(1,128)S(1)}, u32[]{:S(2)}, u32[]{:S(2)}) async-start(f32[8,1,3]{2,1,0:T(1,128)} %broadcast_in_dim.18), calls=%async_computation.4 | async-start | bytes 8192 | tf_op jit(solution)/shard_map/all_to_all | solution.py:15
  243.0 139.7 %all-gather.5.cloned.1.call-start = ((), (), s32[]{:S(2)}) async-start(), calls=%async_computation.8 | async-start | bytes 4718592 | tf_op jit(solution)/shard_map/all_gather | solution.py:32
  246.8 3.8 collective-permute-start.10
  250.6 5.0 %collective-permute-start.11 = (f32[3]{0:T(128)S(1)}, f32[3]{0:T(128)S(1)}, u32[]{:S(2)}, u32[]{:S(2)}) collective-permute-start(f32[3]{0:T(128)S(1)} %add.159), channel_id=1, source_target_pairs={{0,16},{8,24},{16,0},{24,8},{32,48},{40,56},{48,32},{56,40},{64,80... | collective-permute-start | bytes 44 | tf_op jit(solution)/shard_map/ppermute | solution.py:26
  255.6 3.5 collective-permute-start.12
  259.2 4.4 %collective-permute-start.13 = (f32[3]{0:T(128)S(1)}, f32[3]{0:T(128)S(1)}, u32[]{:S(2)}, u32[]{:S(2)}) collective-permute-start(f32[3]{0:T(128)S(1)} %add.161), channel_id=1, source_target_pairs={{0,64},{8,72},{16,80},{24,88},{32,96},{40,104},{48,112},{56,120},{... | collective-permute-start | bytes 44 | tf_op jit(solution)/shard_map/ppermute | solution.py:26
  266.7 9.1 %collective-permute-start.14 = (f32[128,256]{1,0:T(8,128)S(1)}, f32[128,256]{1,0:T(8,128)S(1)}, u32[]{:S(2)}, u32[]{:S(2)}) collective-permute-start(f32[128,256]{1,0:T(8,128)S(1)} %constant_dynamic-slice_fusion), channel_id=1, source_target_pairs={{0,128},{8,136},{16,144},{24,152},{32,160},{40,168},{48,176},{56,1... | collective-permute-start | bytes 393224 | tf_op jit(solution)/shard_map/ppermute | solution.py:26
  286.0 3.6 collective-permute-start.15
  289.6 5.0 %collective-permute-start.16 = (f32[3]{0:T(128)S(1)}, f32[3]{0:T(128)S(1)}, u32[]{:S(2)}, u32[]{:S(2)}) collective-permute-start(f32[3]{0:T(128)S(1)} %add.168), channel_id=1, source_target_pairs={{0,16},{8,24},{16,0},{24,8},{32,48},{40,56},{48,32},{56,40},{64,80... | collective-permute-start | bytes 44 | tf_op jit(solution)/shard_map/ppermute | solution.py:26
  294.7 3.5 collective-permute-start.17
  298.2 4.9 %collective-permute-start.18 = (f32[3]{0:T(128)S(1)}, f32[3]{0:T(128)S(1)}, u32[]{:S(2)}, u32[]{:S(2)}) collective-permute-start(f32[3]{0:T(128)S(1)} %add.170), channel_id=1, source_target_pairs={{0,64},{8,72},{16,80},{24,88},{32,96},{40,104},{48,112},{56,120},{... | collective-permute-start | bytes 44 | tf_op jit(solution)/shard_map/ppermute | solution.py:26
  303.1 7.6 %collective-permute-start.19 = (f32[3]{0:T(128)S(1)}, f32[3]{0:T(128)S(1)}, u32[]{:S(2)}, u32[]{:S(2)}) collective-permute-start(f32[3]{0:T(128)S(1)} %add.171), channel_id=1, source_target_pairs={{0,128},{8,136},{16,144},{24,152},{32,160},{40,168},{48,176},{56,1... | collective-permute-start | bytes 44 | tf_op jit(solution)/shard_map/ppermute | solution.py:26
Sparse Core Ops, SparseCore 0:
  9.8 36.5 all-gather.2
  49.0 53.5 reduce-scatter.1
  327.8 54.7 all-gather.4
where the time goes:
time: 396 us; the launch traced here: 394 us
  waiting for transfers between devices  223 us (56%)
  starting transfers between devices  68.3 us (17%)
  other arithmetic  30.2 us (8%)
  between operations  26.3 us (7%)
  blocking collectives  21.5 us (5%)
  local copies, waits for them, and re-layouts  16 us (4%)
  matrix products  8.93 us (2%)
    ppermute x20, waiting for transfers between devices, swapped(): return lax.ppermute(value, axis, pairs)  122 us
    all_gather x1, waiting for transfers between devices, gather_axes(): nearer = lax.all_gather(shard, axes[-1], axis=dim, tiled=True)  52.8 us
    ppermute x20, starting transfers between devices, swapped(): return lax.ppermute(value, axis, pairs)  49.5 us
    all_gather x1, waiting for transfers between devices, on_device(): lax.all_gather(attention, 'tensor', axis=1, tiled=True)  32.2 us
    all_to_all x4, starting transfers between devices, from_everyone(): return lax.all_to_all(copies, axis, split_axis=0, concat_axis=0, tiled=True)  18.8 us
    all_to_all x4, waiting for transfers between devices, from_everyone(): return lax.all_to_all(copies, axis, split_axis=0, concat_axis=0, tiled=True)  15 us
    all_gather x1, blocking collectives, gather_axes(): nearer = lax.all_gather(shard, axes[-1], axis=dim, tiled=True)  13.9 us
    reduce_sum x5, other arithmetic, halving_merge(): jnp.sum(lower_vec * lower_vec)  13.2 us
  transfers between devices with their start and end apart: 27, of which 26 were waited for; matrix products, arithmetic and copies ran while one was open for 12% of the time, Pallas kernels for 0%

commit v1 on v0

v1 whole, which is shorter than its diff:
```python
import jax
import jax.numpy as jnp
from jax import lax
from jax.sharding import Mesh
from jax.sharding import PartitionSpec as P

EPS = 1e-06


def tree_weights(gram, n):
    g = [[gram[i, j] for j in range(n)] for i in range(n)]
    w = [jnp.float32(1.0)] * n
    span = 1
    while len(g) > 1:
        half = len(g) // 2
        c = []
        for i in range(half):
            aa, bb, s = g[2 * i][2 * i], g[2 * i + 1][2 * i + 1], g[2 * i][2 * i + 1]
            c.append(1.0 - s / (2.0 * (aa + EPS)))
            c.append(1.0 - s / (2.0 * (bb + EPS)))
        w = [w[k] * c[k // span] for k in range(n)]
        span *= 2
        g = [
            [
                sum(c[a] * c[b] * g[a][b] for a in (2 * i, 2 * i + 1) for b in (2 * j, 2 * j + 1))
                for j in range(half)
            ]
            for i in range(half)
        ]
    return w


def merged(parts, axes):
    n = parts.shape[0]
    flat = [parts[i] for i in range(n)]
    dots = jnp.stack([jnp.sum(flat[i] * flat[j]) for i in range(n) for j in range(i, n)])
    dots = lax.psum(dots, axes)
    idx = {}
    k = 0
    for i in range(n):
        for j in range(i, n):
            idx[i, j] = idx[j, i] = dots[k]
            k += 1
    w = tree_weights(idx, n)
    return sum(w[i] * flat[i] for i in range(n))


def on_device(attention, cotangent, projection):
    full = lax.all_gather(cotangent, "tensor", axis=1, tiled=True)
    rows = lax.all_to_all(projection, "tensor", split_axis=0, concat_axis=1, tiled=True)
    input_grad = lax.dot_general(
        full, rows, (((1,), (1,)), ((), ())), preferred_element_type=jnp.float32
    ).astype(jnp.bfloat16)
    grad = lax.dot_general(
        attention, full, (((0,), (0,)), ((), ())), preferred_element_type=jnp.float32
    )
    parts = lax.all_to_all(grad.reshape(4, 128, 2048), "dp_1", 0, 0, tiled=True)
    quarter = merged(parts, ("dp_1", "tensor"))
    parts = lax.all_to_all(quarter.reshape(8, 16, 2048), "dp_0", 0, 0, tiled=True)
    piece = merged(parts, ("dp_0", "dp_1", "tensor"))
    piece = piece.reshape(16, 8, 256).transpose(1, 0, 2)
    piece = lax.all_to_all(piece, "tensor", 0, 0, tiled=True)
    gathered = lax.all_gather(piece, ("dp_0", "dp_1"), axis=0)
    combined = gathered.reshape(8, 4, 8, 16, 256).transpose(2, 1, 0, 3, 4).reshape(4096, 256)
    return (input_grad, combined)


def solution(mesh):
    finer = Mesh(mesh.devices.reshape(8, 4, mesh.shape["tensor"]), ("dp_0", "dp_1", "tensor"))
    dp = ("dp_0", "dp_1")
    return jax.shard_map(
        on_device,
        mesh=finer,
        in_specs=(P(dp, "tensor"), P(dp, "tensor"), P(None, "tensor")),
        out_specs=(P(dp, "tensor"), P(None, "tensor")),
        check_vma=False,
    )
```

time: 396 us -> 450 us (1.14)
  blocking collectives: 21.5 us -> 263 us
  waiting for transfers between devices: 223 us -> 74.7 us
  starting transfers between devices: 68.3 us -> 0.08 us
  between operations: 26.3 us -> 58 us
  other arithmetic: 30.2 us -> 6.32 us
  local copies, waits for them, and re-layouts: 16 us -> 39 us
    psum x0 -> x2, blocking collectives: none -> 136 us  [merged(): dots = lax.psum(dots, axes)]
    ppermute x20 -> x0, waiting for transfers between devices: 122 us -> none  [swapped(): return lax.ppermute(value, axis, pairs)]
    all_to_all x1 -> x4, blocking collectives: 7.61 us -> 128 us  [the longest x1 53.3 us: on_device(): parts = lax.all_to_all(grad.reshape(4, 128, 2048), 'dp_1', 0, 0, tiled=True)]
    ppermute x20 -> x0, starting transfers between devices: 49.5 us -> none  [swapped(): return lax.ppermute(value, axis, pairs)]
    another operation x0 -> x2, local copies, waits for them, and re-layouts: none -> 29.5 us  [merged(): jnp.stack([jnp.sum(flat[i] * flat[j]) for i in range(n) for j in range(i,...]
    all_to_all x4 -> x0, starting transfers between devices: 18.8 us -> none  [from_everyone(): return lax.all_to_all(copies, axis, split_axis=0, concat_axis=0, tiled=True)]
    all_to_all x4 -> x0, waiting for transfers between devices: 15 us -> none  [from_everyone(): return lax.all_to_all(copies, axis, split_axis=0, concat_axis=0, tiled=True)]
    all_gather x1 -> x0, blocking collectives: 13.9 us -> none  [gather_axes(): nearer = lax.all_gather(shard, axes[-1], axis=dim, tiled=True)]
  transfers between devices with their start and end apart: 27 -> 2, of which waited for: 26 -> 2; matrix products, arithmetic and copies ran while one was open for 12% -> 1% of each run, Pallas kernels for 0% -> 0%
where the time goes in v1:
time: 450 us; the launch traced here: 449 us
  blocking collectives  263 us (58%)
  waiting for transfers between devices  74.7 us (17%)
  between operations  58 us (13%)
  local copies, waits for them, and re-layouts  39 us (9%)
  matrix products  7.15 us (2%)
  other arithmetic  6.32 us (1%)
    psum x2, blocking collectives, merged(): dots = lax.psum(dots, axes)  136 us
    all_to_all x1, blocking collectives, on_device(): parts = lax.all_to_all(grad.reshape(4, 128, 2048), 'dp_1', 0, 0, tiled=True)  53.3 us
    all_gather x1, waiting for transfers between devices, on_device(): gathered = lax.all_gather(piece, ('dp_0', 'dp_1'), axis=0)  39.9 us
    all_to_all x1, blocking collectives, on_device(): lax.all_to_all(quarter.reshape(8, 16, 2048), 'dp_0', 0, 0, tiled=True)  34.2 us
    all_gather x1, waiting for transfers between devices, on_device(): full = lax.all_gather(cotangent, 'tensor', axis=1, tiled=True)  34.1 us
    all_to_all x1, blocking collectives, on_device(): lax.all_to_all(projection, 'tensor', split_axis=0, concat_axis=1, tiled=T...  31 us
    another operation x2, local copies, waits for them, and re-layouts, merged(): jnp.stack([jnp.sum(flat[i] * flat[j]) for i in range(n) for j in range(i,...  29.5 us
    all_to_all x1, blocking collectives, on_device(): piece = lax.all_to_all(piece, 'tensor', 0, 0, tiled=True)  9.09 us
  transfers between devices with their start and end apart: 2, of which 2 were waited for; matrix products, arithmetic and copies ran while one was open for 1% of the time, Pallas kernels for 0%

profile of v1, /device:TPU:2, one launch (start us, length us, event | category | flops | bytes accessed | tf_op | source)
XLA Modules:
  0.0 448.7 jit_solution(10173290104913362302)
XLA Ops:
  7.2 0.0 copy-start
  7.2 0.0 all-gather.4.cloned.1.call-start
  7.2 0.7 all-gather.4.cloned.1.call-update
  7.9 0.0 all-gather.6.cloned.1.call-start
  8.0 34.1 %all-gather.4.cloned.1.call-done = bf16[512,2048]{1,0:T(8,128)(2,1)} async-done(((bf16[512,256]{1,0:T(8,128)(2,1)}), bf16[512,2048]{1,0:T(8,128)(2,1)}) %all-gather.4.cloned.1.call-update) | async-done | bytes 2097168 | tf_op jit(solution)/shard_map/all_gather | solution.py:49
  42.1 0.0 copy-done
  42.1 2.9 fusion.3
  45.0 53.3 %all_to_all.34 = f32[4,128,2048]{2,1,0:T(8,128)S(1)} all-to-all(f32[4,128,2048]{2,1,0:T(8,128)S(1)} %bitcast.110), channel_id=1, replica_groups=mesh['dp_0'=8,'dp_1'=4,'tensor'=8] {'dp_1'}, dimensions={0} | all-to-all | bytes 8388608 | tf_op jit(solution)/shard_map/all_to_all | solution.py:57
  98.3 0.0 copy-start.1
  98.3 2.0 multiply_reduce_fusion
  100.3 0.0 copy-done.1
  100.3 6.3 %stack.154 = f32[10]{0:T(128)S(1)} concatenate(f32[1]{0:T(128)} %bitcast.4, f32[1]{0:T(128)} %bitcast.5, f32[1]{0:T(128)} %bitcast.6, f32[1]{0:T(128)} %bitcast.7, f32[1]{0:T(128)} %bitcast.8, f32[1]{0:T(128)} %bitcast.9, f32[1]{0:T(128)} %bitcast.10, f32[1]{0:T(128)} %bitcast.11, f32[1]{0:T(128)} %bitcast.12, f32[1]{0:T(128)} %bitcast.13), dimensions={0} | concatenate | bytes 80 | tf_op jit(solution)/shard_map/stack | solution.py:36
  106.6 59.5 %psum.14 = f32[10]{0:T(128)S(1)} all-reduce(f32[10]{0:T(128)S(1)} %stack.154), channel_id=1, replica_groups=mesh['dp_0'=8,'dp_1'=4,'tensor'=8] {'dp_1','tensor'}, use_global_device_ids=true, to_apply=%region_10.0 | all-reduce | flops 10 | bytes 80 | tf_op jit(solution)/shard_map/psum | solution.py:37
  166.1 0.7 fusion.2
  177.8 2.5 multiply_add_fusion
  180.3 34.2 %all_to_all.35 = f32[8,16,2048]{2,1,0:T(8,128)S(1)} all-to-all(f32[8,16,2048]{2,1,0:T(8,128)S(1)} %bitcast.112), channel_id=1, replica_groups=mesh['dp_0'=8,'dp_1'=4,'tensor'=8] {'dp_0'}, dimensions={0} | all-to-all | bytes 2097152 | tf_op jit(solution)/shard_map/all_to_all | solution.py:59
  214.5 0.8 multiply_reduce_fusion.10
  215.3 0.9 multiply_reduce_fusion.11
  216.3 23.3 %stack.191 = f32[36]{0:T(128)S(1)} concatenate(f32[1]{0:T(128)} %bitcast.25, f32[1]{0:T(128)} %bitcast.26, f32[1]{0:T(128)} %bitcast.27, f32[1]{0:T(128)} %bitcast.28, f32[1]{0:T(128)} %bitcast.29, f32[1]{0:T(128)} %bitcast.30, f32[1]{0:T(128)} %bitcast.31, f32[1]{0:T(128)} %bitcast.32, f32[1]{0:T(128)} %bitcast.33, f32[1]{0:T(128)} %bitcast.34, f32[1]{0:T(128)} %bitcast.35, ...), dimensions={0} | concatenate | bytes 288 | tf_op jit(solution)/shard_map/stack | solution.py:36
  239.5 76.3 %psum.15 = f32[36]{0:T(128)S(1)} all-reduce(f32[36]{0:T(128)S(1)} %stack.191), channel_id=1, replica_groups=mesh['dp_0'=8,'dp_1'=4,'tensor'=8] {'dp_0','dp_1','tensor'}, use_global_device_ids=true, to_apply=%region_47.0 | all-reduce | flops 36 | bytes 288 | tf_op jit(solution)/shard_map/psum | solution.py:37
  315.9 0.7 fusion.1
  331.7 0.7 fusion
  350.1 0.1 add_add_fusion
  350.3 9.1 %all_to_all.36 = f32[8,16,256]{2,1,0:T(8,128)} all-to-all(f32[8,16,256]{2,1,0:T(8,128)S(1)} %copy.12), channel_id=1, replica_groups=mesh['dp_0'=8,'dp_1'=4,'tensor'=8] {'tensor'}, dimensions={0} | all-to-all | bytes 262144 | tf_op jit(solution)/shard_map/all_to_all | solution.py:62
  359.4 0.0 all-gather.6.cloned.1.call-update
  359.4 31.0 %all_to_all.37 = bf16[8,512,256]{2,1,0:T(8,128)(2,1)S(1)} all-to-all(bf16[8,512,256]{2,1,0:T(8,128)(2,1)} %bitcast.115), channel_id=1, replica_groups=mesh['dp_0'=8,'dp_1'=4,'tensor'=8] {'tensor'}, dimensions={0} | all-to-all | bytes 4194304 | tf_op jit(solution)/shard_map/all_to_all | solution.py:50
  390.5 2.4 copy.11
  392.9 4.3 convolution_convert_fusion
  397.1 39.9 %all-gather.6.cloned.1.call-done = f32[256,16,256]{2,1,0:T(8,128)} async-done(((f32[8,16,256]{2,1,0:T(8,128)}), f32[256,16,256]{2,1,0:T(8,128)}) %all-gather.6.cloned.1.call-update) | async-done | bytes 4194320 | tf_op jit(solution)/shard_map/all_gather | solution.py:63
  437.0 4.8 %copy.13 = f32[8,4,8,16,256]{4,3,2,1,0:T(8,128)} copy(f32[8,4,8,16,256]{4,3,0,1,2:T(8,128)} %bitcast.113) | data formatting | bytes 8388608 | tf_op jit(solution)/shard_map/transpose | solution.py:64
  (2 shorter events, 0.1 us)
Async XLA Ops:
  7.2 34.9 %copy-start = (bf16[512,512]{1,0:T(8,128)(2,1)S(1)}, bf16[512,512]{1,0:T(8,128)(2,1)}, u32[]{:S(2)}) copy-start(bf16[512,512]{1,0:T(8,128)(2,1)} %param.3) | copy-start | bytes 1572868
  7.2 34.9 %all-gather.4.cloned.1.call-start = ((), (), s32[]{:S(2)}) async-start(), calls=%async_computation.4 | async-start | bytes 2359296 | tf_op jit(solution)/shard_map/all_gather | solution.py:49
  7.9 429.1 %all-gather.6.cloned.1.call-start = ((), (), s32[]{:S(2)}) async-start(), calls=%async_computation.5 | async-start | bytes 4325376 | tf_op jit(solution)/shard_map/all_gather | solution.py:63
  98.3 2.0 copy-start.1
Sparse Core Ops, SparseCore 0:
  9.8 32.2 all-gather.3
  359.6 77.3 all-gather.5

commit v2 on v1

v2 whole, which is shorter than its diff:
```python
import jax
import jax.numpy as jnp
from jax import lax
from jax.experimental import pallas as pl
from jax.experimental.pallas import tpu as pltpu
from jax.sharding import PartitionSpec as P

EPS = 1e-06
MESH = pl.DeviceIdType.MESH
NX, NC, NY, NZ = 4, 2, 4, 8
NT = NX * NC
F32 = jnp.float32
BF16 = jnp.bfloat16
CUT = 80


def pairs(n):
    return [(i, j) for i in range(n) for j in range(i, n)]


def tree_weights(rows, n):
    table = {}
    for k, (i, j) in enumerate(pairs(n)):
        table[i, j] = table[j, i] = rows[k]
    weights = [None] * n
    span, m = 1, n
    while m > 1:
        half = m // 2
        coef = []
        for i in range(half):
            aa = jnp.maximum(table[2 * i, 2 * i], 0.0)
            bb = jnp.maximum(table[2 * i + 1, 2 * i + 1], 0.0)
            s = table[2 * i, 2 * i + 1]
            coef.append(1.0 - s / (2.0 * (aa + EPS)))
            coef.append(1.0 - s / (2.0 * (bb + EPS)))
        for k in range(n):
            c = coef[k // span]
            weights[k] = c if weights[k] is None else weights[k] * c
        if half > 1:
            new = {}
            for i in range(half):
                for j in range(i, half):
                    if i == j:
                        a, b = 2 * i, 2 * i + 1
                        v = (
                            coef[a] * coef[a] * table[a, a]
                            + coef[b] * coef[b] * table[b, b]
                            + 2.0 * (coef[a] * coef[b] * table[a, b])
                        )
                    else:
                        v = coef[2 * i] * (
                            coef[2 * j] * table[2 * i, 2 * j]
                            + coef[2 * j + 1] * table[2 * i, 2 * j + 1]
                        ) + coef[2 * i + 1] * (
                            coef[2 * j] * table[2 * i + 1, 2 * j]
                            + coef[2 * j + 1] * table[2 * i + 1, 2 * j + 1]
                        )
                    new[i, j] = new[j, i] = v
            table = new
        span, m = span * 2, half
    return weights


def body(
    att,
    cot,
    proj,
    igrad,
    comb,
    s1,
    ab,
    cb,
    cf,
    pb,
    g,
    mz,
    rz,
    st1,
    sr1,
    sr2,
    st2,
    tr1,
    tr2,
    tr3,
    fin,
    loc,
    a1s,
    a1r,
    b1s,
    b1r,
    c1s,
    c1r,
    cys,
    cyr,
    cfs,
    cfr,
    pbs,
    pbr,
    g1s,
    g1r,
    g2s,
    g2r,
    zs,
    zr,
    h1s,
    h1r,
    h2s,
    h2r,
    h3s,
    h3r,
    f1zs,
    f1zr,
    f1ys,
    f1yr,
    f2ys,
    f2yr,
    f2zs,
    f2zr,
):
    dp = lax.axis_index("dp")
    t = lax.axis_index("tensor")
    z, y = lax.div(dp, NY), lax.rem(dp, NY)
    x, c = lax.div(t, NC), lax.rem(t, NC)
    turn = 1 - 2 * c
    sib = 1 - c

    def xi(d):
        return lax.rem(x + d + NX, NX)

    def yi(d):
        return lax.rem(y + d + NY, NY)

    def zi(d):
        return lax.rem(z + d + NZ, NZ)

    def dev(z_=None, y_=None, t_=None):
        z_ = z if z_ is None else z_
        y_ = y if y_ is None else y_
        t_ = t if t_ is None else t_
        return {"dp": z_ * NY + y_, "tensor": t_}

    def copy(src, dst, ss, rs, to):
        return pltpu.make_async_remote_copy(
            src_ref=src, dst_ref=dst, send_sem=ss, recv_sem=rs, device_id=to, device_id_type=MESH
        )

    sent = []

    def send(src, dst, ss, rs, to):
        d = copy(src, dst, ss, rs, to)
        d.start()
        sent.append(d)

    def arrived(ref, ss, rs):
        copy(ref, ref, ss, rs, dev()).wait_recv()

    barrier = pltpu.get_barrier_semaphore()
    for j in range(1, NT):
        pl.semaphore_signal(barrier, 1, device_id=dev(t_=lax.rem(t + j, NT)), device_id_type=MESH)
    for j in range(1, NY):
        pl.semaphore_signal(barrier, 1, device_id=dev(y_=yi(j)), device_id_type=MESH)
    for j in range(1, NZ):
        pl.semaphore_signal(barrier, 1, device_id=dev(z_=zi(j)), device_id_type=MESH)
    own = [
        pltpu.make_async_copy(att.at[t], s1.at[t], loc.at[0]),
        pltpu.make_async_copy(cot, cb.at[y], loc.at[1]),
        pltpu.make_async_copy(cot, cf.at[t], loc.at[2]),
        pltpu.make_async_copy(proj.at[t], pb.at[t], loc.at[3]),
    ]
    for d in own:
        d.start()
    pl.semaphore_wait(barrier, (NT - 1) + (NY - 1) + (NZ - 1))

    for j in (4, 5, 3, 2, 6, 1, 7):
        to = lax.rem(t + j, NT)
        send(att.at[to], s1.at[t], a1s.at[j], a1r.at[t], dev(t_=to))
    send(cot, cb.at[y], cys.at[0], cyr.at[y], dev(y_=yi(1)))
    send(cot, cb.at[y], cys.at[1], cyr.at[y], dev(y_=yi(-1)))
    own[0].wait()
    for j in range(1, NT):
        s = lax.rem(t + j, NT)
        arrived(s1.at[s], a1s.at[0], a1r.at[s])
    for j in (2, 1, 3):
        q = yi(j)
        send(s1.at[pl.ds(2 * q, 2)], ab.at[t, y], b1s.at[j], b1r.at[y], dev(y_=q))
    mine = pltpu.make_async_copy(s1.at[pl.ds(2 * y, 2)], ab.at[t, y], loc.at[4])
    mine.start()
    yb, yf = yi(-turn), yi(turn)
    arrived(cb.at[yb], cys.at[0], cyr.at[yb])
    send(cb.at[yb], cb.at[yb], cys.at[2], cyr.at[yb], dev(y_=yf))
    for j in range(1, NY):
        q = yi(j)
        arrived(ab.at[t, q], b1s.at[0], b1r.at[q])
    mine.wait()

    class RowGather:
        def __init__(self, buf, ss, rs, first):
            self.buf, self.ss, self.rs = buf, ss, rs
            self.put(first, t, 0, NC * xi(1) + c)
            self.put(first, t, 1, NC * xi(-1) + c)
            self.put(first, t, 2, NC * x + sib)

        def put(self, src, slot, k, to):
            send(src, self.buf.at[slot], self.ss.at[k], self.rs.at[slot], dev(t_=to))

        def got(self, slot):
            arrived(self.buf.at[slot], self.ss.at[0], self.rs.at[slot])

        def forward(self):
            xb, xf = NC * xi(-turn) + c, NC * xi(turn) + c
            self.got(xb)
            self.put(self.buf.at[xb], xb, 3, xf)
            self.put(self.buf.at[xb], xb, 4, NC * x + sib)
            self.got(xf)
            self.put(self.buf.at[xf], xf, 5, NC * x + sib)

        def last(self):
            x2 = NC * xi(2) + c
            self.got(x2)
            self.put(self.buf.at[x2], x2, 6, NC * x + sib)

        def finish(self):
            for j in range(NX):
                self.got(NC * xi(j) + sib)

    rows = RowGather(ab, c1s, c1r, ab.at[t])
    rows.forward()
    rows.last()
    own[1].wait()
    arrived(cb.at[yf], cys.at[0], cyr.at[yf])
    y2 = yi(2)
    arrived(cb.at[y2], cys.at[0], cyr.at[y2])
    rows.finish()

    def grad(i, _):
        r, h = lax.div(i, 2), lax.rem(i, 2)
        a = ab[:, r, h].reshape(512, 512)
        v = lax.dot_general(cb[r], a, (((0,), (0,)), ((), ())), preferred_element_type=F32)
        for k in range(4):
            g[r, 4 * h + k] = v[:, 128 * k : 128 * (k + 1)]
        return 0

    lax.fori_loop(0, 8, grad, 0)

    def dots(load, n, steps, out):
        pn = pairs(n)

        def one(i, acc):
            v = [load(k, i) for k in range(n)]
            return tuple(a + v[p] * v[q] for a, (p, q) in zip(acc, pn))

        acc = lax.fori_loop(
            0, steps, one, tuple(jnp.zeros((8, 128), F32) for _ in pn), unroll=2
        )
        for k, a in enumerate(acc):
            out[k : k + 1, :] = jnp.sum(a, axis=0, keepdims=True)

    def load_g(k, i):
        return g[k, lax.div(i, 32), pl.ds(pl.multiple_of(lax.rem(i, 32) * 8, 8), 8), :]

    st1[...] = jnp.zeros_like(st1)
    dots(load_g, NY, 256, st1)

    def share(buf, slot, ss, rs, count, index, where):
        for j in range(1, count):
            send(buf.at[slot], buf.at[slot], ss.at[j], rs.at[slot], where(index(j)))
        for j in range(1, count):
            k = index(j)
            arrived(buf.at[k], ss.at[0], rs.at[k])
        total = buf[0]
        for k in range(1, count):
            total = total + buf[k]
        return total

    def ti(j):
        return lax.rem(t + j, NT)

    def full_rows(total, n):
        lanes = jnp.broadcast_to(jnp.sum(total, axis=1, keepdims=True), total.shape)
        return [lanes[k : k + 1, :] for k in range(len(pairs(n)))]

    sr1[t] = st1[...]
    sr2[y] = share(sr1, t, g1s, g1r, NT, ti, lambda k: dev(t_=k))
    total = share(sr2, y, g2s, g2r, NY, yi, lambda k: dev(y_=k))
    w = tree_weights(full_rows(total, NY), NY)

    def merge_into(dst, load, ws):
        def one(i, _):
            at = pl.ds(pl.multiple_of(i * 8, 8), 8)
            v = load(0, at) * ws[0]
            for k in range(1, len(ws)):
                v = v + load(k, at) * ws[k]
            dst[at, :] = v
            return 0

        lax.fori_loop(0, 32, one, 0)

    for j in (4, 3, 5, 2, 6, 1, 7, 0):
        zz = zi(j)
        merge_into(
            rz.at[z] if j == 0 else mz.at[zz], lambda k, at, zz=zz: g[k, zz, at, :], w
        )
        if j:
            send(mz.at[zz], rz.at[z], zs.at[j], zr.at[z], dev(z_=zz))

    cots = RowGather(cf, cfs, cfr, cot)
    for j in (1, 2, 3):
        send(proj.at[ti(j)], pb.at[t], pbs.at[j], pbr.at[t], dev(t_=ti(j)))
    cots.forward()
    cots.last()

    for j in range(1, NZ):
        k = zi(j)
        arrived(rz.at[k], zs.at[0], zr.at[k])

    def load_r(k, i):
        return rz[k, pl.ds(pl.multiple_of(i * 8, 8), 8), :]

    st2[...] = jnp.zeros_like(st2)
    dots(load_r, NZ, 32, st2)
    tr1[t] = st2[...]
    tr2[y] = share(tr1, t, h1s, h1r, NT, ti, lambda k: dev(t_=k))
    tr3[z] = share(tr2, y, h2s, h2r, NY, yi, lambda k: dev(y_=k))
    total = share(tr3, z, h3s, h3r, NZ, zi, lambda k: dev(z_=k))
    w = tree_weights(full_rows(total, NZ), NZ)
    merge_into(mz.at[z], lambda k, at: rz[k, at, :], w)
    fin[y, z] = jnp.transpose(mz[z])

    upper, lower = pl.ds(0, CUT), pl.ds(CUT, 128 - CUT)

    def f1z(zz, k, to):
        r = fin.at[y, zz, upper]
        send(r, r, f1zs.at[k], f1zr.at[zz], dev(z_=to))

    def f1z_got(zz):
        arrived(fin.at[y, zz, upper], f1zs.at[0], f1zr.at[zz])

    def f1y(yy, zz, k, to):
        r = fin.at[yy, zz, upper]
        send(r, r, f1ys.at[k, zz], f1yr.at[yy, zz], dev(y_=to))

    def f1y_got(yy, zz):
        arrived(fin.at[yy, zz, upper], f1ys.at[0, 0], f1yr.at[yy, zz])

    def f1y_start(zz):
        f1y(y, zz, 0, yf)
        f1y(y, zz, 1, yb)

    def f1y_forward(zz):
        f1y_got(yb, zz)
        f1y(yb, zz, 2, yf)

    def f2y(yy, k, to):
        r = fin.at[yy, z, lower]
        send(r, r, f2ys.at[k], f2yr.at[yy], dev(y_=to))

    def f2y_got(yy):
        arrived(fin.at[yy, z, lower], f2ys.at[0], f2yr.at[yy])

    def f2z(zz, k, to):
        r = fin.at[:, zz, lower]
        send(r, r, f2zs.at[k], f2zr.at[zz], dev(z_=to))

    def f2z_got(zz):
        arrived(fin.at[:, zz, lower], f2zs.at[0], f2zr.at[zz])

    zf, zb = zi(turn), zi(-turn)
    f1z(z, 0, zf)
    f1z(z, 1, zb)
    f2y(y, 0, yf)
    f2y(y, 1, yb)
    f1y_start(z)
    f2y_got(yb)
    f2y(yb, 2, yf)
    f2y_got(yf)
    for j in (4, 5, 6, 7):
        send(proj.at[ti(j)], pb.at[t], pbs.at[j], pbr.at[t], dev(t_=ti(j)))
    f1z_got(zb)
    f1z(zb, 2, zf)
    f1z_got(zf)
    f1z(zf, 3, zb)
    f2y_got(y2)
    f2z(z, 0, zf)
    f2z(z, 1, zb)
    f1y_start(zb)
    f1y_start(zf)
    f1y_forward(z)
    zb2, zf2 = zi(-2 * turn), zi(2 * turn)
    f1z_got(zb2)
    f1z(zb2, 4, zf)
    f1z_got(zf2)
    f1z(zf2, 5, zb)
    f1y_start(zb2)
    f1y_start(zf2)
    f2z_got(zb)
    f2z(zb, 2, zf)
    f2z_got(zf)
    f2z(zf, 3, zb)
    f1y_forward(zb)
    f1y_forward(zf)
    zb3, zf3, z4 = zi(-3 * turn), zi(3 * turn), zi(4)
    f1z_got(zb3)
    f1z(zb3, 6, zf)
    f1z_got(zf3)
    f1y_start(zb3)
    f1y_start(zf3)
    f1y_forward(zb2)
    f1y_forward(zf2)
    f2z_got(zb2)
    f2z(zb2, 4, zf)
    f2z_got(zf2)
    f2z(zf2, 5, zb)
    f1z_got(z4)
    f1y_start(z4)
    f1y_forward(zb3)
    f1y_forward(zf3)
    f2z_got(zb3)
    f2z(zb3, 6, zf)
    f1y_forward(z4)

    own[2].wait()
    own[3].wait()
    cots.finish()
    for j in range(1, NT):
        k = ti(j)
        arrived(pb.at[k], pbs.at[0], pbr.at[k])

    def part(i, _):
        at = pl.ds(pl.multiple_of(i * 128, 128), 128)
        v = jnp.zeros((128, 512), F32)
        for k in range(NT):
            v = v + lax.dot_general(
                cf[k, at, :], pb[k], (((1,), (1,)), ((), ())), preferred_element_type=F32
            )
        igrad[at, :] = v.astype(BF16)
        return 0

    lax.fori_loop(0, 4, part, 0)

    f2z_got(zf3)
    f2z_got(z4)
    for j in range(NZ):
        zz = zi(j)
        f1y_got(yf, zz)
        f1y_got(y2, zz)
    out = pltpu.make_async_copy(fin, comb, loc.at[5])
    out.start()
    for d in sent:
        d.wait_send()
    out.wait()


def on_device(attention, cotangent, projection):
    dma = pltpu.SemaphoreType.DMA
    v = pltpu.VMEM
    igrad, comb = pl.pallas_call(
        body,
        out_shape=(
            jax.ShapeDtypeStruct((512, 512), BF16),
            jax.ShapeDtypeStruct((NY, NZ, 128, 256), F32),
        ),
        in_specs=[pl.BlockSpec(memory_space=pl.ANY)] * 3,
        out_specs=(
            pl.BlockSpec(memory_space=pltpu.VMEM),
            pl.BlockSpec(memory_space=pl.ANY),
        ),
        scratch_shapes=[
            v((NT, 64, 512), BF16),
            v((NT, NY, 2, 64, 512), BF16),
            v((NY, 512, 256), BF16),
            v((NT, 512, 256), BF16),
            v((NT, 512, 256), BF16),
            v((NY, NZ, 256, 128), F32),
            v((NZ, 256, 128), F32),
            v((NZ, 256, 128), F32),
            v((16, 128), F32),
            v((NT, 16, 128), F32),
            v((NY, 16, 128), F32),
            v((40, 128), F32),
            v((NT, 40, 128), F32),
            v((NY, 40, 128), F32),
            v((NZ, 40, 128), F32),
            v((NY, NZ, 128, 256), F32),
            dma((6,)),
            dma((NT,)),
            dma((NT,)),
            dma((NY,)),
            dma((NY,)),
            dma((7,)),
            dma((NT,)),
            dma((3,)),
            dma((NY,)),
            dma((7,)),
            dma((NT,)),
            dma((NT,)),
            dma((NT,)),
            dma((NT,)),
            dma((NT,)),
            dma((NY,)),
            dma((NY,)),
            dma((NZ,)),
            dma((NZ,)),
            dma((NT,)),
            dma((NT,)),
            dma((NY,)),
            dma((NY,)),
            dma((NZ,)),
            dma((NZ,)),
            dma((7,)),
            dma((NZ,)),
            dma((3, NZ)),
            dma((NY, NZ)),
            dma((3,)),
            dma((NY,)),
            dma((7,)),
            dma((NZ,)),
        ],
        compiler_params=pltpu.CompilerParams(
            collective_id=0, has_side_effects=True, vmem_limit_bytes=48 * 1024 * 1024
        ),
        cost_estimate=pl.CostEstimate(
            flops=4 * 2**30, bytes_accessed=16 * 2**20, transcendentals=0
        ),
    )(
        attention.reshape(NT, 64, 512),
        cotangent,
        projection.reshape(NT, 512, 256),
    )
    return (igrad, comb.reshape(4096, 256))


def solution(mesh):
    return jax.shard_map(
        on_device,
        mesh=mesh,
        in_specs=(P("dp", "tensor"), P("dp", "tensor"), P(None, "tensor")),
        out_specs=(P("dp", "tensor"), P(None, "tensor")),
        check_vma=False,
    )
```

time: 450 us -> 143 us (0.32)
  blocking collectives: 263 us -> 0 us
  Pallas kernels: 0 us -> 133 us
  waiting for transfers between devices: 74.7 us -> 0 us
  between operations: 58 us -> 0.65 us
  local copies, waits for them, and re-layouts: 39 us -> 8.84 us
  matrix products: 7.15 us -> 0 us
  other arithmetic: 6.32 us -> 0 us
    psum x2 -> x0, blocking collectives: 136 us -> none  [merged(): dots = lax.psum(dots, axes)]
    pallas_call x0 -> x1, Pallas kernels: none -> 133 us  [on_device(): pl.pallas_call(body, out_shape=(jax.ShapeDtypeStruct((512, 512), BF16), j...]
    all_to_all x4 -> x0, blocking collectives: 128 us -> none  [the longest x1 53.3 us: on_device(): parts = lax.all_to_all(grad.reshape(4, 128, 2048), 'dp_1', 0, 0, tiled=True)]
    all_gather x2 -> x0, waiting for transfers between devices: 74 us -> none  [the longest x1 39.9 us: on_device(): gathered = lax.all_gather(piece, ('dp_0', 'dp_1'), axis=0)]
    another operation x2 -> x0, local copies, waits for them, and re-layouts: 29.5 us -> none  [merged(): jnp.stack([jnp.sum(flat[i] * flat[j]) for i in range(n) for j in range(i,...]
    unnamed x5 -> x8, local copies, waits for them, and re-layouts: 0.07 us -> 8.84 us
    dot_general x2 -> x0, matrix products: 7.15 us -> none  [the longest x1 4.27 us: on_device(): lax.dot_general(full, rows, (((1,), (1,)), ((), ())), preferred_element_t...]
    transpose x2 -> x0, local copies, waits for them, and re-layouts: 4.89 us -> none  [the longest x1 4.84 us: on_device(): gathered.reshape(8, 4, 8, 16, 256).transpose(2, 1, 0, 3, 4)]
  transfers between devices with their start and end apart: 2 -> 0, of which waited for: 2 -> 0; matrix products, arithmetic and copies ran while one was open for 1% -> 0% of each run, Pallas kernels for 0% -> 0%
where the time goes in v2:
time: 143 us; the launch traced here: 142 us
  Pallas kernels  133 us (93%)
  local copies, waits for them, and re-layouts  8.84 us (6%)
    pallas_call x1, Pallas kernels, on_device(): pl.pallas_call(body, out_shape=(jax.ShapeDtypeStruct((512, 512), BF16), j...  133 us
    unnamed x8, local copies, waits for them, and re-layouts  8.84 us

profile of v2, /device:TPU:2, one launch (start us, length us, event | category | flops | bytes accessed | tf_op | source)
XLA Modules:
  0.0 142.1 jit_solution(1398950818287661160)
XLA Ops:
  0.6 0.0 copy-start
  0.6 1.6 %copy-done = bf16[4096,256]{1,0:T(8,128)(2,1)S(1)} copy-done((bf16[4096,256]{1,0:T(8,128)(2,1)S(1)}, bf16[4096,256]{1,0:T(8,128)(2,1)}, u32[]{:S(2)}) %copy-start) | copy-done | bytes 2097176
  2.2 0.0 copy-start.1
  2.2 1.0 copy-done.1
  3.3 0.0 copy-start.2
  3.3 0.9 copy-done.2
  4.2 132.7 %shard_map.50 = (bf16[512,512]{1,0:T(8,128)(2,1)S(1)}, f32[4,8,128,256]{3,2,1,0:T(8,128)}) custom-call(bf16[8,64,512]{2,1,0:T(8,128)(2,1)S(1)} %bitcast.4, bf16[512,256]{1,0:T(8,128)(2,1)S(1)} %copy-done.2, bf16[8,512,256]{2,1,0:T(8,128)(2,1)S(1)} %bitcast.3), custom_call_target="tpu_custom_call" | custom-call | flops 4294967296 | bytes 16777216 | tf_op jit(solution)/shard_map/pallas_call | solution.py:456
  136.9 0.8 copy.7
  137.7 4.5 %copy.8 = f32[4096,256]{1,0:T(8,128)} copy(f32[4096,256]{1,0:T(8,128)} %bitcast.5) | data formatting | bytes 8388608
Async XLA Ops:
  0.6 1.6 %copy-start = (bf16[4096,256]{1,0:T(8,128)(2,1)S(1)}, bf16[4096,256]{1,0:T(8,128)(2,1)}, u32[]{:S(2)}) copy-start(bf16[4096,256]{1,0:T(8,128)(2,1)} %param.5) | copy-start | bytes 6291460
  2.2 1.0 copy-start.1
  3.3 0.9 copy-start.2

commit v3 on v2

--- a/solution.py
+++ b/solution.py
@@ -66,7 +66,7 @@
     cot,
     proj,
     igrad,
-    comb,
+    fin,
     s1,
     ab,
     cb,
@@ -82,7 +82,6 @@
     tr1,
     tr2,
     tr3,
-    fin,
     loc,
     a1s,
     a1r,
@@ -94,8 +93,10 @@
     cyr,
     cfs,
     cfr,
-    pbs,
-    pbr,
+    pxs,
+    pxr,
+    pzs,
+    pzr,
     g1s,
     g1r,
     g2s,
@@ -162,36 +163,20 @@
     for j in range(1, NZ):
         pl.semaphore_signal(barrier, 1, device_id=dev(z_=zi(j)), device_id_type=MESH)
     own = [
-        pltpu.make_async_copy(att.at[t], s1.at[t], loc.at[0]),
-        pltpu.make_async_copy(cot, cb.at[y], loc.at[1]),
-        pltpu.make_async_copy(cot, cf.at[t], loc.at[2]),
-        pltpu.make_async_copy(proj.at[t], pb.at[t], loc.at[3]),
+        pltpu.make_async_copy(att.at[0, t], s1.at[0, t], loc.at[0]),
+        pltpu.make_async_copy(att.at[1, t], s1.at[1, t], loc.at[1]),
+        pltpu.make_async_copy(cot, cb.at[y], loc.at[2]),
+        pltpu.make_async_copy(cot, cf.at[t], loc.at[3]),
+        pltpu.make_async_copy(proj.at[t, z], pb.at[z, t], loc.at[4]),
     ]
     for d in own:
         d.start()
     pl.semaphore_wait(barrier, (NT - 1) + (NY - 1) + (NZ - 1))
 
-    for j in (4, 5, 3, 2, 6, 1, 7):
-        to = lax.rem(t + j, NT)
-        send(att.at[to], s1.at[t], a1s.at[j], a1r.at[t], dev(t_=to))
-    send(cot, cb.at[y], cys.at[0], cyr.at[y], dev(y_=yi(1)))
-    send(cot, cb.at[y], cys.at[1], cyr.at[y], dev(y_=yi(-1)))
-    own[0].wait()
-    for j in range(1, NT):
-        s = lax.rem(t + j, NT)
-        arrived(s1.at[s], a1s.at[0], a1r.at[s])
-    for j in (2, 1, 3):
-        q = yi(j)
-        send(s1.at[pl.ds(2 * q, 2)], ab.at[t, y], b1s.at[j], b1r.at[y], dev(y_=q))
-    mine = pltpu.make_async_copy(s1.at[pl.ds(2 * y, 2)], ab.at[t, y], loc.at[4])
-    mine.start()
-    yb, yf = yi(-turn), yi(turn)
-    arrived(cb.at[yb], cys.at[0], cyr.at[yb])
-    send(cb.at[yb], cb.at[yb], cys.at[2], cyr.at[yb], dev(y_=yf))
-    for j in range(1, NY):
-        q = yi(j)
-        arrived(ab.at[t, q], b1s.at[0], b1r.at[q])
-    mine.wait()
+    def ti(j):
+        return lax.rem(t + j, NT)
+
+    yb, yf, y2 = yi(-turn), yi(turn), yi(2)
 
     class RowGather:
         def __init__(self, buf, ss, rs, first):
@@ -223,24 +208,105 @@
             for j in range(NX):
                 self.got(NC * xi(j) + sib)
 
-    rows = RowGather(ab, c1s, c1r, ab.at[t])
-    rows.forward()
-    rows.last()
-    own[1].wait()
+    class DepthRing:
+        def __init__(self, block, ss, rs):
+            self.block, self.ss, self.rs = block, ss, rs
+            self.put(z, 0, zi(turn))
+            self.put(z, 1, zi(-turn))
+
+        def put(self, zz, k, to):
+            r = self.block(zz)
+            send(r, r, self.ss.at[k], self.rs.at[zz], dev(z_=to))
+
+        def got(self, zz):
+            arrived(self.block(zz), self.ss.at[0], self.rs.at[zz])
+
+        def far(self, h):
+            zz = zi(-h * turn)
+            self.got(zz)
+            if h < 4:
+                self.put(zz, 2 * h, zi(turn))
+            return zz
+
+        def near(self, h):
+            zz = zi(h * turn)
+            self.got(zz)
+            if h < 3:
+                self.put(zz, 2 * h + 1, zi(-turn))
+            return zz
+
+    for h in range(2):
+        for j in (4, 5, 3, 2, 6, 1, 7):
+            to = ti(j)
+            send(att.at[h, to], s1.at[h, t], a1s.at[h, j], a1r.at[h, t], dev(t_=to))
+    send(cot, cb.at[y], cys.at[0], cyr.at[y], dev(y_=yi(1)))
+    send(cot, cb.at[y], cys.at[1], cyr.at[y], dev(y_=yi(-1)))
+    for j in (4, 5, 3, 2, 6, 1, 7):
+        to = ti(j)
+        send(proj.at[to, z], pb.at[z, t], pxs.at[j], pxr.at[t], dev(t_=to))
+    mine = []
+    for h in range(2):
+        own[h].wait()
+        for j in range(1, NT):
+            s = ti(j)
+            arrived(s1.at[h, s], a1s.at[h, 0], a1r.at[h, s])
+        for j in (2, 1, 3):
+            q = yi(j)
+            send(s1.at[h, pl.ds(2 * q, 2)], ab.at[h, t, y], b1s.at[h, j], b1r.at[h, y], dev(y_=q))
+        mine.append(
+            pltpu.make_async_copy(s1.at[h, pl.ds(2 * y, 2)], ab.at[h, t, y], loc.at[5 + h])
+        )
+        mine[h].start()
+
+    def row_ready(h):
+        for j in range(1, NY):
+            q = yi(j)
+            arrived(ab.at[h, t, q], b1s.at[h, 0], b1r.at[h, q])
+        mine[h].wait()
+        return RowGather(ab.at[h], c1s.at[h], c1r.at[h], ab.at[h, t])
+
+    rows0 = row_ready(0)
+    own[4].wait()
+    for j in range(1, NT):
+        k = ti(j)
+        arrived(pb.at[z, k], pxs.at[0], pxr.at[k])
+    depth = DepthRing(lambda zz: pb.at[zz], pzs, pzr)
+    arrived(cb.at[yb], cys.at[0], cyr.at[yb])
+    send(cb.at[yb], cb.at[yb], cys.at[2], cyr.at[yb], dev(y_=yf))
+    rows1 = row_ready(1)
+    rows0.forward()
+    rows1.forward()
+    own[2].wait()
     arrived(cb.at[yf], cys.at[0], cyr.at[yf])
-    y2 = yi(2)
     arrived(cb.at[y2], cys.at[0], cyr.at[y2])
-    rows.finish()
-
-    def grad(i, _):
-        r, h = lax.div(i, 2), lax.rem(i, 2)
-        a = ab[:, r, h].reshape(512, 512)
-        v = lax.dot_general(cb[r], a, (((0,), (0,)), ((), ())), preferred_element_type=F32)
-        for k in range(4):
-            g[r, 4 * h + k] = v[:, 128 * k : 128 * (k + 1)]
-        return 0
-
-    lax.fori_loop(0, 8, grad, 0)
+    rows0.last()
+    depth.far(1)
+    depth.near(1)
+    rows0.finish()
+
+    def grad(h):
+        def one(i, _):
+            r, b = lax.div(i, 2), lax.rem(i, 2)
+            a = ab[h, :, r, b].reshape(256, 512)
+            v = lax.dot_general(
+                cb[r, 256 * h : 256 * (h + 1), :],
+                a,
+                (((0,), (0,)), ((), ())),
+                preferred_element_type=F32,
+            )
+            for k in range(4):
+                u = v[:, 128 * k : 128 * (k + 1)]
+                g[r, 4 * b + k] = u if h == 0 else g[r, 4 * b + k] + u
+            return 0
+
+        lax.fori_loop(0, 8, one, 0)
+
+    grad(0)
+    rows1.last()
+    rows1.finish()
+    grad(1)
+    depth.far(2)
+    depth.near(2)
 
     def dots(load, n, steps, out):
         pn = pairs(n)
@@ -272,16 +338,15 @@
             total = total + buf[k]
         return total
 
-    def ti(j):
-        return lax.rem(t + j, NT)
-
     def full_rows(total, n):
         lanes = jnp.broadcast_to(jnp.sum(total, axis=1, keepdims=True), total.shape)
         return [lanes[k : k + 1, :] for k in range(len(pairs(n)))]
 
     sr1[t] = st1[...]
     sr2[y] = share(sr1, t, g1s, g1r, NT, ti, lambda k: dev(t_=k))
+    cots = RowGather(cf, cfs, cfr, cot)
     total = share(sr2, y, g2s, g2r, NY, yi, lambda k: dev(y_=k))
+    depth.far(3)
     w = tree_weights(full_rows(total, NY), NY)
 
     def merge_into(dst, load, ws):
@@ -303,11 +368,26 @@
         if j:
             send(mz.at[zz], rz.at[z], zs.at[j], zr.at[z], dev(z_=zz))
 
-    cots = RowGather(cf, cfs, cfr, cot)
-    for j in (1, 2, 3):
-        send(proj.at[ti(j)], pb.at[t], pbs.at[j], pbr.at[t], dev(t_=ti(j)))
     cots.forward()
     cots.last()
+    depth.near(3)
+    depth.far(4)
+    own[3].wait()
+    cots.finish()
+
+    def part(i, _):
+        k0, k1 = lax.div(i, 4), lax.rem(i, 4)
+        at = pl.ds(pl.multiple_of(k0 * 256, 256), 256)
+        v = jnp.zeros((256, 128), F32)
+        for k in range(NT):
+            b = pb[pl.ds(2 * k1, 2), k].reshape(128, 256)
+            v = v + lax.dot_general(
+                cf[k, at, :], b, (((1,), (1,)), ((), ())), preferred_element_type=F32
+            )
+        igrad[at, pl.ds(pl.multiple_of(k1 * 128, 128), 128)] = v.astype(BF16)
+        return 0
+
+    lax.fori_loop(0, 8, part, 0)
 
     for j in range(1, NZ):
         k = zi(j)
@@ -328,13 +408,6 @@
 
     upper, lower = pl.ds(0, CUT), pl.ds(CUT, 128 - CUT)
 
-    def f1z(zz, k, to):
-        r = fin.at[y, zz, upper]
-        send(r, r, f1zs.at[k], f1zr.at[zz], dev(z_=to))
-
-    def f1z_got(zz):
-        arrived(fin.at[y, zz, upper], f1zs.at[0], f1zr.at[zz])
-
     def f1y(yy, zz, k, to):
         r = fin.at[yy, zz, upper]
         send(r, r, f1ys.at[k, zz], f1yr.at[yy, zz], dev(y_=to))
@@ -357,101 +430,44 @@
     def f2y_got(yy):
         arrived(fin.at[yy, z, lower], f2ys.at[0], f2yr.at[yy])
 
-    def f2z(zz, k, to):
-        r = fin.at[:, zz, lower]
-        send(r, r, f2zs.at[k], f2zr.at[zz], dev(z_=to))
-
-    def f2z_got(zz):
-        arrived(fin.at[:, zz, lower], f2zs.at[0], f2zr.at[zz])
-
-    zf, zb = zi(turn), zi(-turn)
-    f1z(z, 0, zf)
-    f1z(z, 1, zb)
+    ring1 = DepthRing(lambda zz: fin.at[y, zz, upper], f1zs, f1zr)
     f2y(y, 0, yf)
     f2y(y, 1, yb)
     f1y_start(z)
     f2y_got(yb)
     f2y(yb, 2, yf)
     f2y_got(yf)
-    for j in (4, 5, 6, 7):
-        send(proj.at[ti(j)], pb.at[t], pbs.at[j], pbr.at[t], dev(t_=ti(j)))
-    f1z_got(zb)
-    f1z(zb, 2, zf)
-    f1z_got(zf)
-    f1z(zf, 3, zb)
     f2y_got(y2)
-    f2z(z, 0, zf)
-    f2z(z, 1, zb)
-    f1y_start(zb)
-    f1y_start(zf)
-    f1y_forward(z)
-    zb2, zf2 = zi(-2 * turn), zi(2 * turn)
-    f1z_got(zb2)
-    f1z(zb2, 4, zf)
-    f1z_got(zf2)
-    f1z(zf2, 5, zb)
-    f1y_start(zb2)
-    f1y_start(zf2)
-    f2z_got(zb)
-    f2z(zb, 2, zf)
-    f2z_got(zf)
-    f2z(zf, 3, zb)
-    f1y_forward(zb)
-    f1y_forward(zf)
-    zb3, zf3, z4 = zi(-3 * turn), zi(3 * turn), zi(4)
-    f1z_got(zb3)
-    f1z(zb3, 6, zf)
-    f1z_got(zf3)
-    f1y_start(zb3)
-    f1y_start(zf3)
-    f1y_forward(zb2)
-    f1y_forward(zf2)
-    f2z_got(zb2)
-    f2z(zb2, 4, zf)
-    f2z_got(zf2)
-    f2z(zf2, 5, zb)
-    f1z_got(z4)
-    f1y_start(z4)
-    f1y_forward(zb3)
-    f1y_forward(zf3)
-    f2z_got(zb3)
-    f2z(zb3, 6, zf)
-    f1y_forward(z4)
-
-    own[2].wait()
-    own[3].wait()
-    cots.finish()
-    for j in range(1, NT):
-        k = ti(j)
-        arrived(pb.at[k], pbs.at[0], pbr.at[k])
-
-    def part(i, _):
-        at = pl.ds(pl.multiple_of(i * 128, 128), 128)
-        v = jnp.zeros((128, 512), F32)
-        for k in range(NT):
-            v = v + lax.dot_general(
-                cf[k, at, :], pb[k], (((1,), (1,)), ((), ())), preferred_element_type=F32
-            )
-        igrad[at, :] = v.astype(BF16)
-        return 0
-
-    lax.fori_loop(0, 4, part, 0)
-
-    f2z_got(zf3)
-    f2z_got(z4)
+    ring2 = DepthRing(lambda zz: fin.at[:, zz, lower], f2zs, f2zr)
+    done = [z]
+    for h in range(1, 5):
+        new = [ring1.far(h)]
+        if h < 4:
+            new.append(ring1.near(h))
+        for zz in new:
+            f1y_start(zz)
+        for zz in done:
+            f1y_forward(zz)
+        done = new
+        ring2.far(h)
+        if h < 4:
+            ring2.near(h)
+    for zz in done:
+        f1y_forward(zz)
     for j in range(NZ):
         zz = zi(j)
         f1y_got(yf, zz)
         f1y_got(y2, zz)
-    out = pltpu.make_async_copy(fin, comb, loc.at[5])
-    out.start()
     for d in sent:
         d.wait_send()
-    out.wait()
 
 
 def on_device(attention, cotangent, projection):
     dma = pltpu.SemaphoreType.DMA
+
+    def hbm(a):
+        return pltpu.with_memory_space_constraint(a, pltpu.HBM)
+
     v = pltpu.VMEM
     igrad, comb = pl.pallas_call(
         body,
@@ -462,14 +478,14 @@
         in_specs=[pl.BlockSpec(memory_space=pl.ANY)] * 3,
         out_specs=(
             pl.BlockSpec(memory_space=pltpu.VMEM),
-            pl.BlockSpec(memory_space=pl.ANY),
+            pl.BlockSpec(memory_space=pltpu.VMEM),
         ),
         scratch_shapes=[
-            v((NT, 64, 512), BF16),
-            v((NT, NY, 2, 64, 512), BF16),
+            v((2, NT, 32, 512), BF16),
+            v((2, NT, NY, 2, 32, 512), BF16),
             v((NY, 512, 256), BF16),
             v((NT, 512, 256), BF16),
-            v((NT, 512, 256), BF16),
+            v((NZ, NT, 64, 256), BF16),
             v((NY, NZ, 256, 128), F32),
             v((NZ, 256, 128), F32),
             v((NZ, 256, 128), F32),
@@ -480,20 +496,21 @@
             v((NT, 40, 128), F32),
             v((NY, 40, 128), F32),
             v((NZ, 40, 128), F32),
-            v((NY, NZ, 128, 256), F32),
-            dma((6,)),
-            dma((NT,)),
-            dma((NT,)),
-            dma((NY,)),
-            dma((NY,)),
             dma((7,)),
-            dma((NT,)),
+            dma((2, NT)),
+            dma((2, NT)),
+            dma((2, NY)),
+            dma((2, NY)),
+            dma((2, 7)),
+            dma((2, NT)),
             dma((3,)),
             dma((NY,)),
             dma((7,)),
             dma((NT,)),
             dma((NT,)),
             dma((NT,)),
+            dma((8,)),
+            dma((NZ,)),
             dma((NT,)),
             dma((NT,)),
             dma((NY,)),
@@ -522,9 +539,9 @@
             flops=4 * 2**30, bytes_accessed=16 * 2**20, transcendentals=0
         ),
     )(
-        attention.reshape(NT, 64, 512),
-        cotangent,
-        projection.reshape(NT, 512, 256),
+        hbm(attention.reshape(2, NT, 32, 512)),
+        hbm(cotangent),
+        hbm(projection.reshape(NT, NZ, 64, 256)),
     )
     return (igrad, comb.reshape(4096, 256))
 

time: 143 us -> 135 us (0.944)
  local copies, waits for them, and re-layouts: 8.84 us -> 2.81 us
  Pallas kernels: 133 us -> 131 us
    unnamed x8 -> x2, local copies, waits for them, and re-layouts: 8.84 us -> 2.81 us
    pallas_call x1, Pallas kernels: 133 us -> 131 us  [on_device(): pl.pallas_call(body, out_shape=(jax.ShapeDtypeStruct((512, 512), BF16), j...]
where the time goes in v3:
time: 135 us; the launch traced here: 134 us
  Pallas kernels  131 us (97%)
  local copies, waits for them, and re-layouts  2.81 us (2%)
    pallas_call x1, Pallas kernels, on_device(): pl.pallas_call(body, out_shape=(jax.ShapeDtypeStruct((512, 512), BF16), j...  131 us
    unnamed x2, local copies, waits for them, and re-layouts  2.81 us

profile of v3, /device:TPU:2, one launch (start us, length us, event | category | flops | bytes accessed | tf_op | source)
XLA Modules:
  0.0 134.4 jit_solution(12077752996036580581)
XLA Ops:
  0.6 131.0 %shard_map.50 = (bf16[512,512]{1,0:T(8,128)(2,1)S(1)}, f32[4,8,128,256]{3,2,1,0:T(8,128)S(1)}) custom-call(bf16[2,8,32,512]{3,2,1,0:T(8,128)(2,1)} %bitcast.5, bf16[512,256]{1,0:T(8,128)(2,1)} %cot.1, bf16[8,8,64,256]{3,2,1,0:T(8,128)(2,1)} %bitcast.4), custom_call_target="tpu_custom_call" | custom-call | flops 4294967296 | bytes 16777216 | tf_op jit(solution)/shard_map/pallas_call | solution.py:472
  131.6 0.8 copy.7
  132.4 2.0 %copy.8 = f32[4096,256]{1,0:T(8,128)} copy(f32[4096,256]{1,0:T(8,128)S(1)} %bitcast.3) | data formatting | bytes 8388608

commit v4 on v3

--- a/solution.py
+++ b/solution.py
@@ -1,3 +1,5 @@
+import math
+
 import jax
 import jax.numpy as jnp
 from jax import lax
@@ -11,7 +13,25 @@
 NT = NX * NC
 F32 = jnp.float32
 BF16 = jnp.bfloat16
-CUT = 80
+CUT = 96
+
+
+MU_Z = 2.0**10 - 1
+MU_F = 2.0**18 - 1
+
+
+def encode(v, inv, mu):
+    k = jnp.log(1.0 + jnp.abs(v) * (inv * mu)) * (240.0 / math.log(1.0 + mu)) - 120.0
+    e = jnp.exp2(k)
+    return jnp.where(v < 0, -e, e).astype(BF16)
+
+
+def decode(q, scale, mu):
+    q = q.astype(F32)
+    a = math.log(1.0 + mu) / 240.0
+    h = jnp.log(jnp.abs(q)) * (a / math.log(2.0)) + 120.0 * a
+    u = (jnp.exp(h) - 1.0) * (scale * (1.0 / mu))
+    return jnp.where(q < 0, -u, u)
 
 
 def pairs(n):
@@ -75,13 +95,14 @@
     g,
     mz,
     rz,
-    st1,
-    sr1,
-    sr2,
-    st2,
+    qz,
+    rq,
+    fc,
+    mt,
+    st,
+    sr,
     tr1,
     tr2,
-    tr3,
     loc,
     a1s,
     a1r,
@@ -99,16 +120,12 @@
     pzr,
     g1s,
     g1r,
-    g2s,
-    g2r,
     zs,
     zr,
     h1s,
     h1r,
     h2s,
     h2r,
-    h3s,
-    h3r,
     f1zs,
     f1zr,
     f1ys,
@@ -171,6 +188,7 @@
     ]
     for d in own:
         d.start()
+    st[...] = jnp.zeros_like(st)
     pl.semaphore_wait(barrier, (NT - 1) + (NY - 1) + (NZ - 1))
 
     def ti(j):
@@ -239,8 +257,6 @@
         for j in (4, 5, 3, 2, 6, 1, 7):
             to = ti(j)
             send(att.at[h, to], s1.at[h, t], a1s.at[h, j], a1r.at[h, t], dev(t_=to))
-    send(cot, cb.at[y], cys.at[0], cyr.at[y], dev(y_=yi(1)))
-    send(cot, cb.at[y], cys.at[1], cyr.at[y], dev(y_=yi(-1)))
     for j in (4, 5, 3, 2, 6, 1, 7):
         to = ti(j)
         send(proj.at[to, z], pb.at[z, t], pxs.at[j], pxr.at[t], dev(t_=to))
@@ -257,6 +273,8 @@
             pltpu.make_async_copy(s1.at[h, pl.ds(2 * y, 2)], ab.at[h, t, y], loc.at[5 + h])
         )
         mine[h].start()
+    send(cot, cb.at[y], cys.at[0], cyr.at[y], dev(y_=yi(1)))
+    send(cot, cb.at[y], cys.at[1], cyr.at[y], dev(y_=yi(-1)))
 
     def row_ready(h):
         for j in range(1, NY):
@@ -270,18 +288,22 @@
     for j in range(1, NT):
         k = ti(j)
         arrived(pb.at[z, k], pxs.at[0], pxr.at[k])
-    depth = DepthRing(lambda zz: pb.at[zz], pzs, pzr)
+    depth = [
+        DepthRing(lambda zz, b=b: pb.at[zz, 4 * b : 4 * b + 4], pzs.at[b], pzr.at[b])
+        for b in range(2)
+    ]
+    rows1 = row_ready(1)
+    rows0.forward()
     arrived(cb.at[yb], cys.at[0], cyr.at[yb])
     send(cb.at[yb], cb.at[yb], cys.at[2], cyr.at[yb], dev(y_=yf))
-    rows1 = row_ready(1)
-    rows0.forward()
+    for d in depth:
+        d.far(1)
+        d.near(1)
     rows1.forward()
-    own[2].wait()
-    arrived(cb.at[yf], cys.at[0], cyr.at[yf])
-    arrived(cb.at[y2], cys.at[0], cyr.at[y2])
     rows0.last()
-    depth.far(1)
-    depth.near(1)
+    for d in depth:
+        d.far(2)
+        d.near(2)
     rows0.finish()
 
     def grad(h):
@@ -301,31 +323,42 @@
 
         lax.fori_loop(0, 8, one, 0)
 
+    own[2].wait()
+    arrived(cb.at[yf], cys.at[0], cyr.at[yf])
+    arrived(cb.at[y2], cys.at[0], cyr.at[y2])
     grad(0)
     rows1.last()
+    for d in depth:
+        d.far(3)
     rows1.finish()
     grad(1)
-    depth.far(2)
-    depth.near(2)
-
-    def dots(load, n, steps, out):
+
+    def dots(load, n, steps, top):
         pn = pairs(n)
 
         def one(i, acc):
             v = [load(k, i) for k in range(n)]
-            return tuple(a + v[p] * v[q] for a, (p, q) in zip(acc, pn))
-
+            new = [a + v[p] * v[q] for a, (p, q) in zip(acc, pn)]
+            if top:
+                new += [jnp.maximum(a, jnp.abs(u)) for a, u in zip(acc[len(pn) :], v)]
+            return tuple(new)
+
+        size = len(pn) + (n if top else 0)
         acc = lax.fori_loop(
-            0, steps, one, tuple(jnp.zeros((8, 128), F32) for _ in pn), unroll=2
+            0, steps, one, tuple(jnp.zeros((8, 128), F32) for _ in range(size)), unroll=2
         )
-        for k, a in enumerate(acc):
-            out[k : k + 1, :] = jnp.sum(a, axis=0, keepdims=True)
+        for k, a in enumerate(acc[: len(pn)]):
+            st[k : k + 1, :] = jnp.sum(a, axis=0, keepdims=True)
+        for k, a in enumerate(acc[len(pn) :]):
+            m = jnp.max(jnp.max(a, axis=0, keepdims=True), axis=1, keepdims=True)
+            st[len(pn) + k : len(pn) + k + 1, :] = jnp.broadcast_to(m * (1.0 / 128), (1, 128))
+        row = jnp.sum(jnp.transpose(st[...]), axis=0, keepdims=True)
+        return jnp.broadcast_to(row, (8, 128))
 
     def load_g(k, i):
         return g[k, lax.div(i, 32), pl.ds(pl.multiple_of(lax.rem(i, 32) * 8, 8), 8), :]
 
-    st1[...] = jnp.zeros_like(st1)
-    dots(load_g, NY, 256, st1)
+    local = dots(load_g, NY, 256, False)
 
     def share(buf, slot, ss, rs, count, index, where):
         for j in range(1, count):
@@ -338,40 +371,61 @@
             total = total + buf[k]
         return total
 
-    def full_rows(total, n):
-        lanes = jnp.broadcast_to(jnp.sum(total, axis=1, keepdims=True), total.shape)
-        return [lanes[k : k + 1, :] for k in range(len(pairs(n)))]
-
-    sr1[t] = st1[...]
-    sr2[y] = share(sr1, t, g1s, g1r, NT, ti, lambda k: dev(t_=k))
+    def spread(total, n):
+        return [jnp.broadcast_to(total[0:1, k : k + 1], (1, 128)) for k in range(n)]
+
+    def plane(j):
+        return lax.rem(y * NT + t + j, NY * NT)
+
+    me = y * NT + t
+    sr[me] = local
+    total = share(
+        sr,
+        me,
+        g1s,
+        g1r,
+        NY * NT,
+        plane,
+        lambda k: dev(y_=lax.div(k, NT), t_=lax.rem(k, NT)),
+    )
     cots = RowGather(cf, cfs, cfr, cot)
-    total = share(sr2, y, g2s, g2r, NY, yi, lambda k: dev(y_=k))
-    depth.far(3)
-    w = tree_weights(full_rows(total, NY), NY)
+    w = tree_weights(spread(total, 10), NY)
 
     def merge_into(dst, load, ws):
-        def one(i, _):
+        def one(i, top):
             at = pl.ds(pl.multiple_of(i * 8, 8), 8)
             v = load(0, at) * ws[0]
             for k in range(1, len(ws)):
                 v = v + load(k, at) * ws[k]
             dst[at, :] = v
-            return 0
-
-        lax.fori_loop(0, 32, one, 0)
+            return jnp.maximum(top, jnp.abs(v))
+
+        top = lax.fori_loop(0, 32, one, jnp.zeros((8, 128), F32), unroll=2)
+        return jnp.max(jnp.max(top, axis=0, keepdims=True), axis=1, keepdims=True)
 
     for j in (4, 3, 5, 2, 6, 1, 7, 0):
         zz = zi(j)
-        merge_into(
+        top = merge_into(
             rz.at[z] if j == 0 else mz.at[zz], lambda k, at, zz=zz: g[k, zz, at, :], w
         )
         if j:
-            send(mz.at[zz], rz.at[z], zs.at[j], zr.at[z], dev(z_=zz))
+            scale = jnp.broadcast_to(jnp.maximum(top, 1e-30), (16, 128)).astype(BF16)
+            qz[zz, 256:272, :] = scale
+            inv = 1.0 / scale[0:1, :].astype(F32)
+
+            def code(i, _, zz=zz, inv=inv):
+                at = pl.ds(pl.multiple_of(i * 16, 16), 16)
+                qz[zz, at, :] = encode(mz[zz, at, :], inv, MU_Z)
+                return 0
+
+            lax.fori_loop(0, 16, code, 0, unroll=2)
+            send(qz.at[zz], rq.at[z], zs.at[j], zr.at[z], dev(z_=zz))
 
     cots.forward()
     cots.last()
-    depth.near(3)
-    depth.far(4)
+    for d in depth:
+        d.near(3)
+        d.far(4)
     own[3].wait()
     cots.finish()
 
@@ -389,75 +443,138 @@
 
     lax.fori_loop(0, 8, part, 0)
 
-    for j in range(1, NZ):
+    for j in (1, 7, 2, 6, 3, 5, 4):
         k = zi(j)
-        arrived(rz.at[k], zs.at[0], zr.at[k])
+        arrived(rq.at[k], zs.at[0], zr.at[k])
+        scale = rq[k, 256:272, :].astype(F32)
+
+        def uncode(i, _, k=k, scale=scale):
+            at = pl.ds(pl.multiple_of(i * 16, 16), 16)
+            rz[k, at, :] = decode(rq[k, at, :], scale, MU_Z)
+            return 0
+
+        lax.fori_loop(0, 16, uncode, 0, unroll=2)
 
     def load_r(k, i):
         return rz[k, pl.ds(pl.multiple_of(i * 8, 8), 8), :]
 
-    st2[...] = jnp.zeros_like(st2)
-    dots(load_r, NZ, 32, st2)
-    tr1[t] = st2[...]
-    tr2[y] = share(tr1, t, h1s, h1r, NT, ti, lambda k: dev(t_=k))
-    tr3[z] = share(tr2, y, h2s, h2r, NY, yi, lambda k: dev(y_=k))
-    total = share(tr3, z, h3s, h3r, NZ, zi, lambda k: dev(z_=k))
-    w = tree_weights(full_rows(total, NZ), NZ)
+    tr1[t] = dots(load_r, NZ, 32, True)
+    tr2[dp] = share(tr1, t, h1s, h1r, NT, ti, lambda k: dev(t_=k))
+    total = share(
+        tr2,
+        dp,
+        h2s,
+        h2r,
+        NY * NZ,
+        lambda j: lax.rem(dp + j, NY * NZ),
+        lambda k: {"dp": k, "tensor": t},
+    )
+    rows = spread(total, 44)
+    w = tree_weights(rows, NZ)
     merge_into(mz.at[z], lambda k, at: rz[k, at, :], w)
-    fin[y, z] = jnp.transpose(mz[z])
+    scale = jnp.full((1, 128), 1e-30, F32)
+    for k in range(NZ):
+        scale = scale + jnp.abs(w[k]) * rows[36 + k]
+    scale = scale[0:1, 0:1]
+    inv = 1.0 / scale
+    mt[...] = jnp.transpose(mz[z])
+
+    def code(i, _):
+        at = pl.ds(pl.multiple_of(i * 16, 16), 16)
+        fc[y, z, at, :] = encode(mt[at, :], inv, MU_F)
+        return 0
+
+    lax.fori_loop(0, 8, code, 0, unroll=2)
+
+    def show(yy, zz, low):
+        def one(i, _):
+            at = pl.ds(pl.multiple_of(i * 16, 16), 16)
+            fin[yy, zz, at, :] = decode(fc[yy, zz, at, :], scale, MU_F)
+            return 0
+
+        lo, hi = (CUT // 16, 8) if low else (0, CUT // 16)
+        lax.fori_loop(lo, hi, one, 0, unroll=2)
 
     upper, lower = pl.ds(0, CUT), pl.ds(CUT, 128 - CUT)
 
+    def f1z_got(zz):
+        arrived(fc.at[y, zz, upper], f1zs.at[0], f1zr.at[zz])
+
     def f1y(yy, zz, k, to):
-        r = fin.at[yy, zz, upper]
+        r = fc.at[yy, zz, upper]
         send(r, r, f1ys.at[k, zz], f1yr.at[yy, zz], dev(y_=to))
 
     def f1y_got(yy, zz):
-        arrived(fin.at[yy, zz, upper], f1ys.at[0, 0], f1yr.at[yy, zz])
+        arrived(fc.at[yy, zz, upper], f1ys.at[0, 0], f1yr.at[yy, zz])
 
     def f1y_start(zz):
         f1y(y, zz, 0, yf)
         f1y(y, zz, 1, yb)
+        show(y, zz, False)
 
     def f1y_forward(zz):
         f1y_got(yb, zz)
         f1y(yb, zz, 2, yf)
-
-    def f2y(yy, k, to):
-        r = fin.at[yy, z, lower]
-        send(r, r, f2ys.at[k], f2yr.at[yy], dev(y_=to))
-
-    def f2y_got(yy):
-        arrived(fin.at[yy, z, lower], f2ys.at[0], f2yr.at[yy])
-
-    ring1 = DepthRing(lambda zz: fin.at[y, zz, upper], f1zs, f1zr)
-    f2y(y, 0, yf)
-    f2y(y, 1, yb)
+        show(yb, zz, False)
+
+    def f2z(zz, k, to):
+        r = fc.at[:, zz, lower]
+        send(r, r, f2zs.at[k], f2zr.at[zz], dev(z_=to))
+
+    def f2z_got(zz):
+        arrived(fc.at[:, zz, lower], f2zs.at[0], f2zr.at[zz])
+
+    r = fc.at[y, z, lower]
+    for j in (2, 1, 3):
+        send(r, r, f2ys.at[j], f2yr.at[y], dev(y_=yi(j)))
+    r = fc.at[y, z, upper]
+    for j in (1, 7, 2, 6, 3, 5, 4):
+        send(r, r, f1zs.at[j], f1zr.at[z], dev(z_=zi(j)))
     f1y_start(z)
-    f2y_got(yb)
-    f2y(yb, 2, yf)
-    f2y_got(yf)
-    f2y_got(y2)
-    ring2 = DepthRing(lambda zz: fin.at[:, zz, lower], f2zs, f2zr)
-    done = [z]
-    for h in range(1, 5):
-        new = [ring1.far(h)]
-        if h < 4:
-            new.append(ring1.near(h))
-        for zz in new:
-            f1y_start(zz)
-        for zz in done:
-            f1y_forward(zz)
-        done = new
-        ring2.far(h)
-        if h < 4:
-            ring2.near(h)
-    for zz in done:
-        f1y_forward(zz)
-    for j in range(NZ):
+    for j in range(1, NY):
+        k = yi(j)
+        arrived(fc.at[k, z, lower], f2ys.at[0], f2yr.at[k])
+    f2z(z, 0, zi(turn))
+    f2z(z, 1, zi(-turn))
+    f2z(z, 2, zi(2 * turn))
+    f2z(z, 3, zi(-2 * turn))
+
+    def start(*js):
+        for j in js:
+            f1z_got(zi(j))
+            f1y_start(zi(j))
+
+    start(1, 7)
+    f1y_forward(z)
+    start(2, 6)
+    f2z_got(zi(-2 * turn))
+    f2z(zi(-2 * turn), 4, zi(2 * turn))
+    f2z(zi(-2 * turn), 5, zi(turn))
+    f2z_got(zi(2 * turn))
+    f2z(zi(2 * turn), 6, zi(-turn))
+    f1y_forward(zi(1))
+    f1y_forward(zi(7))
+    start(3, 5)
+    f1y_forward(zi(2))
+    f1y_forward(zi(6))
+    start(4)
+    for j in (3, 5, 4):
+        f1y_forward(zi(j))
+    for k in range(NY):
+        show(k, z, True)
+    for j in (2, 6):
+        for k in range(NY):
+            show(k, zi(j), True)
+    for j in (0, 1, 7, 2, 6, 3, 5, 4):
         zz = zi(j)
         f1y_got(yf, zz)
+        show(yf, zz, False)
         f1y_got(y2, zz)
+        show(y2, zz, False)
+        if j in (1, 7, 3, 5, 4):
+            f2z_got(zz)
+            for k in range(NY):
+                show(k, zz, True)
     for d in sent:
         d.wait_send()
 
@@ -489,13 +606,14 @@
             v((NY, NZ, 256, 128), F32),
             v((NZ, 256, 128), F32),
             v((NZ, 256, 128), F32),
-            v((16, 128), F32),
-            v((NT, 16, 128), F32),
-            v((NY, 16, 128), F32),
-            v((40, 128), F32),
-            v((NT, 40, 128), F32),
-            v((NY, 40, 128), F32),
-            v((NZ, 40, 128), F32),
+            v((NZ, 272, 128), BF16),
+            v((NZ, 272, 128), BF16),
+            v((NY, NZ, 128, 256), BF16),
+            v((128, 256), F32),
+            v((128, 128), F32),
+            v((NY * NT, 8, 128), F32),
+            v((NT, 8, 128), F32),
+            v((NY * NZ, 8, 128), F32),
             dma((7,)),
             dma((2, NT)),
             dma((2, NT)),
@@ -509,25 +627,21 @@
             dma((NT,)),
             dma((NT,)),
             dma((NT,)),
-            dma((8,)),
-            dma((NZ,)),
-            dma((NT,)),
-            dma((NT,)),
-            dma((NY,)),
-            dma((NY,)),
+            dma((2, 8)),
+            dma((2, NZ)),
+            dma((NY * NT,)),
+            dma((NY * NT,)),
             dma((NZ,)),
             dma((NZ,)),
             dma((NT,)),
             dma((NT,)),
-            dma((NY,)),
-            dma((NY,)),
+            dma((NY * NZ,)),
+            dma((NY * NZ,)),
             dma((NZ,)),
-            dma((NZ,)),
-            dma((7,)),
             dma((NZ,)),
             dma((3, NZ)),
             dma((NY, NZ)),
-            dma((3,)),
+            dma((NY,)),
             dma((NY,)),
             dma((7,)),
             dma((NZ,)),

time: 135 us -> 116 us (0.86)
  Pallas kernels: 131 us -> 111 us
    pallas_call x1, Pallas kernels: 131 us -> 111 us  [on_device(): pl.pallas_call(body, out_shape=(jax.ShapeDtypeStruct((512, 512), BF16), j...]
where the time goes in v4:
time: 116 us; the launch traced here: 115 us
  Pallas kernels  111 us (96%)
  local copies, waits for them, and re-layouts  2.81 us (2%)
    pallas_call x1, Pallas kernels, on_device(): pl.pallas_call(body, out_shape=(jax.ShapeDtypeStruct((512, 512), BF16), j...  111 us
    unnamed x2, local copies, waits for them, and re-layouts  2.81 us

profile of v4, /device:TPU:2, one launch (start us, length us, event | category | flops | bytes accessed | tf_op | source)
XLA Modules:
  0.0 114.5 jit_solution(464525891278100416)
XLA Ops:
  0.6 111.1 %shard_map.50 = (bf16[512,512]{1,0:T(8,128)(2,1)S(1)}, f32[4,8,128,256]{3,2,1,0:T(8,128)S(1)}) custom-call(bf16[2,8,32,512]{3,2,1,0:T(8,128)(2,1)} %bitcast.5, bf16[512,256]{1,0:T(8,128)(2,1)} %cot.1, bf16[8,8,64,256]{3,2,1,0:T(8,128)(2,1)} %bitcast.4), custom_call_target="tpu_custom_call" | custom-call | flops 4294967296 | bytes 16777216 | tf_op jit(solution)/shard_map/pallas_call | solution.py:589
  111.7 0.8 copy.7
  112.5 2.0 %copy.8 = f32[4096,256]{1,0:T(8,128)} copy(f32[4096,256]{1,0:T(8,128)S(1)} %bitcast.3) | data formatting | bytes 8388608

commit v5 on v4

--- a/solution.py
+++ b/solution.py
@@ -13,23 +13,25 @@
 NT = NX * NC
 F32 = jnp.float32
 BF16 = jnp.bfloat16
-CUT = 96
-
-
-MU_Z = 2.0**10 - 1
-MU_F = 2.0**18 - 1
+CUT = 112
+
+
+MU_Z = 2.0**8 - 1
+MU_F = 2.0**12 - 1
+TOP = 125.0
+H = 4
 
 
 def encode(v, inv, mu):
-    k = jnp.log(1.0 + jnp.abs(v) * (inv * mu)) * (240.0 / math.log(1.0 + mu)) - 120.0
+    k = jnp.log(1.0 + jnp.abs(v) * (inv * mu)) * (2 * TOP / math.log(1.0 + mu)) - TOP
     e = jnp.exp2(k)
     return jnp.where(v < 0, -e, e).astype(BF16)
 
 
 def decode(q, scale, mu):
     q = q.astype(F32)
-    a = math.log(1.0 + mu) / 240.0
-    h = jnp.log(jnp.abs(q)) * (a / math.log(2.0)) + 120.0 * a
+    a = math.log(1.0 + mu) / (2 * TOP)
+    h = jnp.log(jnp.abs(q)) * (a / math.log(2.0)) + TOP * a
     u = (jnp.exp(h) - 1.0) * (scale * (1.0 / mu))
     return jnp.where(q < 0, -u, u)
 
@@ -180,11 +182,10 @@
     for j in range(1, NZ):
         pl.semaphore_signal(barrier, 1, device_id=dev(z_=zi(j)), device_id_type=MESH)
     own = [
-        pltpu.make_async_copy(att.at[0, t], s1.at[0, t], loc.at[0]),
-        pltpu.make_async_copy(att.at[1, t], s1.at[1, t], loc.at[1]),
-        pltpu.make_async_copy(cot, cb.at[y], loc.at[2]),
-        pltpu.make_async_copy(cot, cf.at[t], loc.at[3]),
-        pltpu.make_async_copy(proj.at[t, z], pb.at[z, t], loc.at[4]),
+        pltpu.make_async_copy(att.at[:, t], s1.at[:, t], loc.at[0]),
+        pltpu.make_async_copy(cot, cb.at[y], loc.at[1]),
+        pltpu.make_async_copy(cot, cf.at[t], loc.at[2]),
+        pltpu.make_async_copy(proj.at[t, z], pb.at[z, t], loc.at[3]),
     ]
     for d in own:
         d.start()
@@ -253,7 +254,7 @@
                 self.put(zz, 2 * h + 1, zi(-turn))
             return zz
 
-    for h in range(2):
+    for h in range(H):
         for j in (4, 5, 3, 2, 6, 1, 7):
             to = ti(j)
             send(att.at[h, to], s1.at[h, t], a1s.at[h, j], a1r.at[h, t], dev(t_=to))
@@ -261,8 +262,8 @@
         to = ti(j)
         send(proj.at[to, z], pb.at[z, t], pxs.at[j], pxr.at[t], dev(t_=to))
     mine = []
-    for h in range(2):
-        own[h].wait()
+    own[0].wait()
+    for h in range(H):
         for j in range(1, NT):
             s = ti(j)
             arrived(s1.at[h, s], a1s.at[h, 0], a1r.at[h, s])
@@ -270,7 +271,7 @@
             q = yi(j)
             send(s1.at[h, pl.ds(2 * q, 2)], ab.at[h, t, y], b1s.at[h, j], b1r.at[h, y], dev(y_=q))
         mine.append(
-            pltpu.make_async_copy(s1.at[h, pl.ds(2 * y, 2)], ab.at[h, t, y], loc.at[5 + h])
+            pltpu.make_async_copy(s1.at[h, pl.ds(2 * y, 2)], ab.at[h, t, y], loc.at[4 + h])
         )
         mine[h].start()
     send(cot, cb.at[y], cys.at[0], cyr.at[y], dev(y_=yi(1)))
@@ -283,8 +284,8 @@
         mine[h].wait()
         return RowGather(ab.at[h], c1s.at[h], c1r.at[h], ab.at[h, t])
 
-    rows0 = row_ready(0)
-    own[4].wait()
+    rows = [row_ready(0), row_ready(1)]
+    own[3].wait()
     for j in range(1, NT):
         k = ti(j)
         arrived(pb.at[z, k], pxs.at[0], pxr.at[k])
@@ -292,24 +293,30 @@
         DepthRing(lambda zz, b=b: pb.at[zz, 4 * b : 4 * b + 4], pzs.at[b], pzr.at[b])
         for b in range(2)
     ]
-    rows1 = row_ready(1)
-    rows0.forward()
+    rows.append(row_ready(2))
+    rows[0].forward()
+    rows.append(row_ready(3))
+    rows[1].forward()
     arrived(cb.at[yb], cys.at[0], cyr.at[yb])
     send(cb.at[yb], cb.at[yb], cys.at[2], cyr.at[yb], dev(y_=yf))
     for d in depth:
         d.far(1)
         d.near(1)
-    rows1.forward()
-    rows0.last()
+    rows[0].last()
+    rows[2].forward()
+    rows[1].last()
+    rows[3].forward()
     for d in depth:
         d.far(2)
         d.near(2)
-    rows0.finish()
+    rows[2].last()
+    rows[0].finish()
+    rows[1].finish()
 
     def grad(h):
         def one(i, _):
             r, b = lax.div(i, 2), lax.rem(i, 2)
-            a = ab[h, :, r, b].reshape(256, 512)
+            a = ab[2 * h : 2 * h + 2, :, r, b].reshape(256, 512)
             v = lax.dot_general(
                 cb[r, 256 * h : 256 * (h + 1), :],
                 a,
@@ -323,14 +330,15 @@
 
         lax.fori_loop(0, 8, one, 0)
 
-    own[2].wait()
+    own[1].wait()
     arrived(cb.at[yf], cys.at[0], cyr.at[yf])
     arrived(cb.at[y2], cys.at[0], cyr.at[y2])
     grad(0)
-    rows1.last()
+    rows[3].last()
     for d in depth:
         d.far(3)
-    rows1.finish()
+    rows[2].finish()
+    rows[3].finish()
     grad(1)
 
     def dots(load, n, steps, top):
@@ -360,16 +368,22 @@
 
     local = dots(load_g, NY, 256, False)
 
-    def share(buf, slot, ss, rs, count, index, where):
+    lane = lax.broadcasted_iota(jnp.int32, (8, 128), 1)
+    maxima = lane >= len(pairs(NZ))
+
+    def share(buf, slot, ss, rs, count, index, where, meanwhile=None):
         for j in range(1, count):
             send(buf.at[slot], buf.at[slot], ss.at[j], rs.at[slot], where(index(j)))
+        if meanwhile is not None:
+            meanwhile()
         for j in range(1, count):
             k = index(j)
             arrived(buf.at[k], ss.at[0], rs.at[k])
-        total = buf[0]
+        total = top = buf[0]
         for k in range(1, count):
             total = total + buf[k]
-        return total
+            top = jnp.maximum(top, buf[k])
+        return jnp.where(maxima, top, total)
 
     def spread(total, n):
         return [jnp.broadcast_to(total[0:1, k : k + 1], (1, 128)) for k in range(n)]
@@ -422,12 +436,26 @@
             send(qz.at[zz], rq.at[z], zs.at[j], zr.at[z], dev(z_=zz))
 
     cots.forward()
+    for j in (1, 7, 2, 6, 3, 5, 4):
+        k = zi(j)
+        arrived(rq.at[k], zs.at[0], zr.at[k])
+        scale = rq[k, 256:272, :].astype(F32)
+
+        def uncode(i, _, k=k, scale=scale):
+            at = pl.ds(pl.multiple_of(i * 16, 16), 16)
+            rz[k, at, :] = decode(rq[k, at, :], scale, MU_Z)
+            return 0
+
+        lax.fori_loop(0, 16, uncode, 0, unroll=2)
+
+    def load_r(k, i):
+        return rz[k, pl.ds(pl.multiple_of(i * 8, 8), 8), :]
+
     cots.last()
     for d in depth:
         d.near(3)
         d.far(4)
-    own[3].wait()
-    cots.finish()
+    own[2].wait()
 
     def part(i, _):
         k0, k1 = lax.div(i, 4), lax.rem(i, 4)
@@ -441,22 +469,9 @@
         igrad[at, pl.ds(pl.multiple_of(k1 * 128, 128), 128)] = v.astype(BF16)
         return 0
 
-    lax.fori_loop(0, 8, part, 0)
-
-    for j in (1, 7, 2, 6, 3, 5, 4):
-        k = zi(j)
-        arrived(rq.at[k], zs.at[0], zr.at[k])
-        scale = rq[k, 256:272, :].astype(F32)
-
-        def uncode(i, _, k=k, scale=scale):
-            at = pl.ds(pl.multiple_of(i * 16, 16), 16)
-            rz[k, at, :] = decode(rq[k, at, :], scale, MU_Z)
-            return 0
-
-        lax.fori_loop(0, 16, uncode, 0, unroll=2)
-
-    def load_r(k, i):
-        return rz[k, pl.ds(pl.multiple_of(i * 8, 8), 8), :]
+    def input_gradient():
+        cots.finish()
+        lax.fori_loop(0, 8, part, 0)
 
     tr1[t] = dots(load_r, NZ, 32, True)
     tr2[dp] = share(tr1, t, h1s, h1r, NT, ti, lambda k: dev(t_=k))
@@ -468,6 +483,7 @@
         NY * NZ,
         lambda j: lax.rem(dp + j, NY * NZ),
         lambda k: {"dp": k, "tensor": t},
+        input_gradient,
     )
     rows = spread(total, 44)
     w = tree_weights(rows, NZ)
@@ -598,8 +614,8 @@
             pl.BlockSpec(memory_space=pltpu.VMEM),
         ),
         scratch_shapes=[
-            v((2, NT, 32, 512), BF16),
-            v((2, NT, NY, 2, 32, 512), BF16),
+            v((H, NT, 16, 512), BF16),
+            v((H, NT, NY, 2, 16, 512), BF16),
             v((NY, 512, 256), BF16),
             v((NT, 512, 256), BF16),
             v((NZ, NT, 64, 256), BF16),
@@ -614,13 +630,13 @@
             v((NY * NT, 8, 128), F32),
             v((NT, 8, 128), F32),
             v((NY * NZ, 8, 128), F32),
-            dma((7,)),
-            dma((2, NT)),
-            dma((2, NT)),
-            dma((2, NY)),
-            dma((2, NY)),
-            dma((2, 7)),
-            dma((2, NT)),
+            dma((8,)),
+            dma((H, NT)),
+            dma((H, NT)),
+            dma((H, NY)),
+            dma((H, NY)),
+            dma((H, 7)),
+            dma((H, NT)),
             dma((3,)),
             dma((NY,)),
             dma((7,)),
@@ -653,7 +669,7 @@
             flops=4 * 2**30, bytes_accessed=16 * 2**20, transcendentals=0
         ),
     )(
-        hbm(attention.reshape(2, NT, 32, 512)),
+        hbm(attention.reshape(H, NT, 16, 512)),
         hbm(cotangent),
         hbm(projection.reshape(NT, NZ, 64, 256)),
     )

time: 116 us -> 112 us (0.966); the launches traced: 115 us -> 112 us
  Pallas kernels: 111 us -> 108 us
    pallas_call x1, Pallas kernels: 111 us -> 108 us  [on_device(): pl.pallas_call(body, out_shape=(jax.ShapeDtypeStruct((512, 512), BF16), j...]
where the time goes in v5:
time: 112 us
  Pallas kernels  108 us (96%)
  local copies, waits for them, and re-layouts  2.81 us (3%)
    pallas_call x1, Pallas kernels, on_device(): pl.pallas_call(body, out_shape=(jax.ShapeDtypeStruct((512, 512), BF16), j...  108 us
    unnamed x2, local copies, waits for them, and re-layouts  2.81 us

profile of v5, /device:TPU:2, one launch (start us, length us, event | category | flops | bytes accessed | tf_op | source)
XLA Modules:
  0.0 111.8 jit_solution(11959822771677343181)
XLA Ops:
  0.6 108.3 %shard_map.50 = (bf16[512,512]{1,0:T(8,128)(2,1)S(1)}, f32[4,8,128,256]{3,2,1,0:T(8,128)S(1)}) custom-call(bf16[4,8,16,512]{3,2,1,0:T(8,128)(2,1)} %bitcast.5, bf16[512,256]{1,0:T(8,128)(2,1)} %cot.1, bf16[8,8,64,256]{3,2,1,0:T(8,128)(2,1)} %bitcast.4), custom_call_target="tpu_custom_call" | custom-call | flops 4294967296 | bytes 16777216 | tf_op jit(solution)/shard_map/pallas_call | solution.py:605
  109.0 0.8 copy.7
  109.8 2.0 %copy.8 = f32[4096,256]{1,0:T(8,128)} copy(f32[4096,256]{1,0:T(8,128)S(1)} %bitcast.3) | data formatting | bytes 8388608

commit v6 on v5

--- a/solution.py
+++ b/solution.py
@@ -118,8 +118,6 @@
     cfr,
     pxs,
     pxr,
-    pzs,
-    pzr,
     g1s,
     g1r,
     zs,
@@ -185,7 +183,7 @@
         pltpu.make_async_copy(att.at[:, t], s1.at[:, t], loc.at[0]),
         pltpu.make_async_copy(cot, cb.at[y], loc.at[1]),
         pltpu.make_async_copy(cot, cf.at[t], loc.at[2]),
-        pltpu.make_async_copy(proj.at[t, z], pb.at[z, t], loc.at[3]),
+        pltpu.make_async_copy(proj.at[t], pb.at[t], loc.at[3]),
     ]
     for d in own:
         d.start()
@@ -227,40 +225,10 @@
             for j in range(NX):
                 self.got(NC * xi(j) + sib)
 
-    class DepthRing:
-        def __init__(self, block, ss, rs):
-            self.block, self.ss, self.rs = block, ss, rs
-            self.put(z, 0, zi(turn))
-            self.put(z, 1, zi(-turn))
-
-        def put(self, zz, k, to):
-            r = self.block(zz)
-            send(r, r, self.ss.at[k], self.rs.at[zz], dev(z_=to))
-
-        def got(self, zz):
-            arrived(self.block(zz), self.ss.at[0], self.rs.at[zz])
-
-        def far(self, h):
-            zz = zi(-h * turn)
-            self.got(zz)
-            if h < 4:
-                self.put(zz, 2 * h, zi(turn))
-            return zz
-
-        def near(self, h):
-            zz = zi(h * turn)
-            self.got(zz)
-            if h < 3:
-                self.put(zz, 2 * h + 1, zi(-turn))
-            return zz
-
     for h in range(H):
         for j in (4, 5, 3, 2, 6, 1, 7):
             to = ti(j)
             send(att.at[h, to], s1.at[h, t], a1s.at[h, j], a1r.at[h, t], dev(t_=to))
-    for j in (4, 5, 3, 2, 6, 1, 7):
-        to = ti(j)
-        send(proj.at[to, z], pb.at[z, t], pxs.at[j], pxr.at[t], dev(t_=to))
     mine = []
     own[0].wait()
     for h in range(H):
@@ -285,30 +253,16 @@
         return RowGather(ab.at[h], c1s.at[h], c1r.at[h], ab.at[h, t])
 
     rows = [row_ready(0), row_ready(1)]
-    own[3].wait()
-    for j in range(1, NT):
-        k = ti(j)
-        arrived(pb.at[z, k], pxs.at[0], pxr.at[k])
-    depth = [
-        DepthRing(lambda zz, b=b: pb.at[zz, 4 * b : 4 * b + 4], pzs.at[b], pzr.at[b])
-        for b in range(2)
-    ]
     rows.append(row_ready(2))
     rows[0].forward()
     rows.append(row_ready(3))
     rows[1].forward()
     arrived(cb.at[yb], cys.at[0], cyr.at[yb])
     send(cb.at[yb], cb.at[yb], cys.at[2], cyr.at[yb], dev(y_=yf))
-    for d in depth:
-        d.far(1)
-        d.near(1)
     rows[0].last()
     rows[2].forward()
     rows[1].last()
     rows[3].forward()
-    for d in depth:
-        d.far(2)
-        d.near(2)
     rows[2].last()
     rows[0].finish()
     rows[1].finish()
@@ -335,8 +289,6 @@
     arrived(cb.at[y2], cys.at[0], cyr.at[y2])
     grad(0)
     rows[3].last()
-    for d in depth:
-        d.far(3)
     rows[2].finish()
     rows[3].finish()
     grad(1)
@@ -452,29 +404,11 @@
         return rz[k, pl.ds(pl.multiple_of(i * 8, 8), 8), :]
 
     cots.last()
-    for d in depth:
-        d.near(3)
-        d.far(4)
-    own[2].wait()
-
-    def part(i, _):
-        k0, k1 = lax.div(i, 4), lax.rem(i, 4)
-        at = pl.ds(pl.multiple_of(k0 * 256, 256), 256)
-        v = jnp.zeros((256, 128), F32)
-        for k in range(NT):
-            b = pb[pl.ds(2 * k1, 2), k].reshape(128, 256)
-            v = v + lax.dot_general(
-                cf[k, at, :], b, (((1,), (1,)), ((), ())), preferred_element_type=F32
-            )
-        igrad[at, pl.ds(pl.multiple_of(k1 * 128, 128), 128)] = v.astype(BF16)
-        return 0
-
-    def input_gradient():
-        cots.finish()
-        lax.fori_loop(0, 8, part, 0)
-
     tr1[t] = dots(load_r, NZ, 32, True)
     tr2[dp] = share(tr1, t, h1s, h1r, NT, ti, lambda k: dev(t_=k))
+    for j in (4, 5, 3, 2, 6, 1, 7):
+        to = ti(j)
+        send(proj.at[to], pb.at[t], pxs.at[j], pxr.at[t], dev(t_=to))
     total = share(
         tr2,
         dp,
@@ -483,7 +417,6 @@
         NY * NZ,
         lambda j: lax.rem(dp + j, NY * NZ),
         lambda k: {"dp": k, "tensor": t},
-        input_gradient,
     )
     rows = spread(total, 44)
     w = tree_weights(rows, NZ)
@@ -544,7 +477,7 @@
     for j in (2, 1, 3):
         send(r, r, f2ys.at[j], f2yr.at[y], dev(y_=yi(j)))
     r = fc.at[y, z, upper]
-    for j in (1, 7, 2, 6, 3, 5, 4):
+    for j in (1, 7, 4, 3, 5, 2, 6):
         send(r, r, f1zs.at[j], f1zr.at[z], dev(z_=zi(j)))
     f1y_start(z)
     for j in range(1, NY):
@@ -562,26 +495,54 @@
 
     start(1, 7)
     f1y_forward(z)
-    start(2, 6)
+    start(4)
+    f1y_forward(zi(1))
+    f1y_forward(zi(7))
+    start(3, 5)
+    f1y_forward(zi(4))
+    for j in (2, 6):
+        zz = zi(j)
+        f1z_got(zz)
+        f1y(y, zz, 2, y2)
+        f1y_start(zz)
     f2z_got(zi(-2 * turn))
     f2z(zi(-2 * turn), 4, zi(2 * turn))
     f2z(zi(-2 * turn), 5, zi(turn))
     f2z_got(zi(2 * turn))
     f2z(zi(2 * turn), 6, zi(-turn))
-    f1y_forward(zi(1))
-    f1y_forward(zi(7))
-    start(3, 5)
-    f1y_forward(zi(2))
-    f1y_forward(zi(6))
-    start(4)
-    for j in (3, 5, 4):
-        f1y_forward(zi(j))
+    f1y_forward(zi(3))
+    f1y_forward(zi(5))
+
+    own[2].wait()
+    own[3].wait()
+    cots.finish()
+    for j in range(1, NT):
+        k = ti(j)
+        arrived(pb.at[k], pxs.at[0], pxr.at[k])
+
+    def part(i, _):
+        k0, k1 = lax.div(i, 4), lax.rem(i, 4)
+        at = pl.ds(pl.multiple_of(k0 * 256, 256), 256)
+        cols = pl.ds(pl.multiple_of(k1 * 128, 128), 128)
+        v = jnp.zeros((256, 128), F32)
+        for k in range(NT):
+            v = v + lax.dot_general(
+                cf[k, at, :], pb[k, cols, :], (((1,), (1,)), ((), ())), preferred_element_type=F32
+            )
+        igrad[at, cols] = v.astype(BF16)
+        return 0
+
+    lax.fori_loop(0, 8, part, 0)
+
+    for j in (2, 6):
+        f1y_got(yb, zi(j))
+        show(yb, zi(j), False)
     for k in range(NY):
         show(k, z, True)
     for j in (2, 6):
         for k in range(NY):
             show(k, zi(j), True)
-    for j in (0, 1, 7, 2, 6, 3, 5, 4):
+    for j in (0, 1, 7, 4, 3, 5, 2, 6):
         zz = zi(j)
         f1y_got(yf, zz)
         show(yf, zz, False)
@@ -618,7 +579,7 @@
             v((H, NT, NY, 2, 16, 512), BF16),
             v((NY, 512, 256), BF16),
             v((NT, 512, 256), BF16),
-            v((NZ, NT, 64, 256), BF16),
+            v((NT, 512, 256), BF16),
             v((NY, NZ, 256, 128), F32),
             v((NZ, 256, 128), F32),
             v((NZ, 256, 128), F32),
@@ -643,8 +604,6 @@
             dma((NT,)),
             dma((NT,)),
             dma((NT,)),
-            dma((2, 8)),
-            dma((2, NZ)),
             dma((NY * NT,)),
             dma((NY * NT,)),
             dma((NZ,)),
@@ -671,7 +630,7 @@
     )(
         hbm(attention.reshape(H, NT, 16, 512)),
         hbm(cotangent),
-        hbm(projection.reshape(NT, NZ, 64, 256)),
+        hbm(projection.reshape(NT, 512, 256)),
     )
     return (igrad, comb.reshape(4096, 256))
 

time: 112 us -> 108 us (0.964); the launches traced: 112 us -> 106 us
  Pallas kernels: 108 us -> 103 us
    pallas_call x1, Pallas kernels: 108 us -> 103 us  [on_device(): pl.pallas_call(body, out_shape=(jax.ShapeDtypeStruct((512, 512), BF16), j...]
where the time goes in v6:
time: 108 us; the launch traced here: 106 us
  Pallas kernels  103 us (95%)
  local copies, waits for them, and re-layouts  2.81 us (3%)
    pallas_call x1, Pallas kernels, on_device(): pl.pallas_call(body, out_shape=(jax.ShapeDtypeStruct((512, 512), BF16), j...  103 us
    unnamed x2, local copies, waits for them, and re-layouts  2.81 us

profile of v6, /device:TPU:2, one launch (start us, length us, event | category | flops | bytes accessed | tf_op | source)
XLA Modules:
  0.0 106.3 jit_solution(4855566077263236275)
XLA Ops:
  0.6 102.8 %shard_map.50 = (bf16[512,512]{1,0:T(8,128)(2,1)S(1)}, f32[4,8,128,256]{3,2,1,0:T(8,128)S(1)}) custom-call(bf16[4,8,16,512]{3,2,1,0:T(8,128)(2,1)} %bitcast.5, bf16[512,256]{1,0:T(8,128)(2,1)} %cot.1, bf16[8,512,256]{2,1,0:T(8,128)(2,1)} %bitcast.4), custom_call_target="tpu_custom_call" | custom-call | flops 4294967296 | bytes 16777216 | tf_op jit(solution)/shard_map/pallas_call | solution.py:566
  103.5 0.8 copy.7
  104.3 2.0 %copy.8 = f32[4096,256]{1,0:T(8,128)} copy(f32[4096,256]{1,0:T(8,128)S(1)} %bitcast.3) | data formatting | bytes 8388608

commit v7 on v6

--- a/solution.py
+++ b/solution.py
@@ -554,6 +554,20 @@
                 show(k, zz, True)
     for d in sent:
         d.wait_send()
+
+
+def leave(igrad, comb, igrad_out, comb_out, sem):
+    copies = [
+        pltpu.make_async_copy(
+            comb.at[1024 * k : 1024 * (k + 1)], comb_out.at[1024 * k : 1024 * (k + 1)], sem.at[k]
+        )
+        for k in range(4)
+    ]
+    copies.append(pltpu.make_async_copy(igrad, igrad_out, sem.at[4]))
+    for d in copies:
+        d.start()
+    for d in copies:
+        d.wait()
 
 
 def on_device(attention, cotangent, projection):
@@ -632,7 +646,21 @@
         hbm(cotangent),
         hbm(projection.reshape(NT, 512, 256)),
     )
-    return (igrad, comb.reshape(4096, 256))
+    return pl.pallas_call(
+        leave,
+        out_shape=(
+            jax.ShapeDtypeStruct((512, 512), BF16),
+            jax.ShapeDtypeStruct((4096, 256), F32),
+        ),
+        in_specs=[pl.BlockSpec(memory_space=pltpu.VMEM)] * 2,
+        out_specs=[pl.BlockSpec(memory_space=pltpu.HBM)] * 2,
+        scratch_shapes=[dma((5,))],
+        compiler_params=pltpu.CompilerParams(vmem_limit_bytes=1024 * 1024),
+        cost_estimate=pl.CostEstimate(flops=0, bytes_accessed=9 * 2**20, transcendentals=0),
+    )(
+        pltpu.with_memory_space_constraint(igrad, pltpu.VMEM),
+        pltpu.with_memory_space_constraint(comb.reshape(4096, 256), pltpu.VMEM),
+    )
 
 
 def solution(mesh):

time: 108 us -> 107 us (level)
  local copies, waits for them, and re-layouts: 2.81 us -> 0 us
  Pallas kernels: 103 us -> 105 us
    unnamed x2 -> x0, local copies, waits for them, and re-layouts: 2.81 us -> none
    pallas_call x0 -> x1, Pallas kernels: none -> 2.22 us  [on_device(): pl.pallas_call(leave, out_shape=(jax.ShapeDtypeStruct((512, 512), BF16),...]
where the time goes in v7:
time: 107 us; the launch traced here: 106 us
  Pallas kernels  105 us (98%)
    pallas_call x1, Pallas kernels, on_device(): pl.pallas_call(body, out_shape=(jax.ShapeDtypeStruct((512, 512), BF16), j...  103 us
    pallas_call x1, Pallas kernels, on_device(): pl.pallas_call(leave, out_shape=(jax.ShapeDtypeStruct((512, 512), BF16),...  2.22 us

profile of v7, /device:TPU:2, one launch (start us, length us, event | category | flops | bytes accessed | tf_op | source)
XLA Modules:
  0.0 105.7 jit_solution(15525188105066738296)
XLA Ops:
  0.6 102.8 %shard_map.50 = (bf16[512,512]{1,0:T(8,128)(2,1)S(1)}, f32[4,8,128,256]{3,2,1,0:T(8,128)S(1)}) custom-call(bf16[4,8,16,512]{3,2,1,0:T(8,128)(2,1)} %bitcast.5, bf16[512,256]{1,0:T(8,128)(2,1)} %cot.1, bf16[8,512,256]{2,1,0:T(8,128)(2,1)} %bitcast.4), custom_call_target="tpu_custom_call" | custom-call | flops 4294967296 | bytes 16777216 | tf_op jit(solution)/shard_map/pallas_call | solution.py:580
  103.5 2.2 %shard_map.51 = (bf16[512,512]{1,0:T(8,128)(2,1)}, f32[4096,256]{1,0:T(8,128)}) custom-call(bf16[512,512]{1,0:T(8,128)(2,1)S(1)} %get-tuple-element.4.igrad, f32[4096,256]{1,0:T(8,128)S(1)} %bitcast.3), custom_call_target="tpu_custom_call" | custom-call | bytes 9437184 | tf_op jit(solution)/shard_map/pallas_call | solution.py:649

commit v8 on v7

--- a/solution.py
+++ b/solution.py
@@ -282,7 +282,7 @@
                 g[r, 4 * b + k] = u if h == 0 else g[r, 4 * b + k] + u
             return 0
 
-        lax.fori_loop(0, 8, one, 0)
+        lax.fori_loop(0, 8, one, 0, unroll=4)
 
     own[1].wait()
     arrived(cb.at[yf], cys.at[0], cyr.at[yf])
@@ -305,7 +305,7 @@
 
         size = len(pn) + (n if top else 0)
         acc = lax.fori_loop(
-            0, steps, one, tuple(jnp.zeros((8, 128), F32) for _ in range(size)), unroll=2
+            0, steps, one, tuple(jnp.zeros((8, 128), F32) for _ in range(size)), unroll=8 if n == NY else 4
         )
         for k, a in enumerate(acc[: len(pn)]):
             st[k : k + 1, :] = jnp.sum(a, axis=0, keepdims=True)
@@ -366,7 +366,7 @@
             dst[at, :] = v
             return jnp.maximum(top, jnp.abs(v))
 
-        top = lax.fori_loop(0, 32, one, jnp.zeros((8, 128), F32), unroll=2)
+        top = lax.fori_loop(0, 32, one, jnp.zeros((8, 128), F32), unroll=8)
         return jnp.max(jnp.max(top, axis=0, keepdims=True), axis=1, keepdims=True)
 
     for j in (4, 3, 5, 2, 6, 1, 7, 0):
@@ -384,7 +384,7 @@
                 qz[zz, at, :] = encode(mz[zz, at, :], inv, MU_Z)
                 return 0
 
-            lax.fori_loop(0, 16, code, 0, unroll=2)
+            lax.fori_loop(0, 16, code, 0, unroll=8)
             send(qz.at[zz], rq.at[z], zs.at[j], zr.at[z], dev(z_=zz))
 
     cots.forward()
@@ -398,7 +398,7 @@
             rz[k, at, :] = decode(rq[k, at, :], scale, MU_Z)
             return 0
 
-        lax.fori_loop(0, 16, uncode, 0, unroll=2)
+        lax.fori_loop(0, 16, uncode, 0, unroll=8)
 
     def load_r(k, i):
         return rz[k, pl.ds(pl.multiple_of(i * 8, 8), 8), :]
@@ -433,7 +433,7 @@
         fc[y, z, at, :] = encode(mt[at, :], inv, MU_F)
         return 0
 
-    lax.fori_loop(0, 8, code, 0, unroll=2)
+    lax.fori_loop(0, 8, code, 0, unroll=8)
 
     def show(yy, zz, low):
         def one(i, _):
@@ -442,7 +442,7 @@
             return 0
 
         lo, hi = (CUT // 16, 8) if low else (0, CUT // 16)
-        lax.fori_loop(lo, hi, one, 0, unroll=2)
+        lax.fori_loop(lo, hi, one, 0, unroll=hi - lo)
 
     upper, lower = pl.ds(0, CUT), pl.ds(CUT, 128 - CUT)
 

time: 107 us -> 104 us (0.972)
  Pallas kernels: 105 us -> 101 us
    pallas_call x1, Pallas kernels: 103 us -> 99.2 us  [on_device(): pl.pallas_call(body, out_shape=(jax.ShapeDtypeStruct((512, 512), BF16), j...]
where the time goes in v8:
time: 104 us; the launch traced here: 102 us
  Pallas kernels  101 us (97%)
    pallas_call x1, Pallas kernels, on_device(): pl.pallas_call(body, out_shape=(jax.ShapeDtypeStruct((512, 512), BF16), j...  99.2 us
    pallas_call x1, Pallas kernels, on_device(): pl.pallas_call(leave, out_shape=(jax.ShapeDtypeStruct((512, 512), BF16),...  2.22 us

profile of v8, /device:TPU:2, one launch (start us, length us, event | category | flops | bytes accessed | tf_op | source)
XLA Modules:
  0.0 102.1 jit_solution(17379703528328193943)
XLA Ops:
  0.6 99.2 %shard_map.50 = (bf16[512,512]{1,0:T(8,128)(2,1)S(1)}, f32[4,8,128,256]{3,2,1,0:T(8,128)S(1)}) custom-call(bf16[4,8,16,512]{3,2,1,0:T(8,128)(2,1)} %bitcast.5, bf16[512,256]{1,0:T(8,128)(2,1)} %cot.1, bf16[8,512,256]{2,1,0:T(8,128)(2,1)} %bitcast.4), custom_call_target="tpu_custom_call" | custom-call | flops 4294967296 | bytes 16777216 | tf_op jit(solution)/shard_map/pallas_call | solution.py:580
  99.9 2.2 %shard_map.51 = (bf16[512,512]{1,0:T(8,128)(2,1)}, f32[4096,256]{1,0:T(8,128)}) custom-call(bf16[512,512]{1,0:T(8,128)(2,1)S(1)} %get-tuple-element.4.igrad, f32[4096,256]{1,0:T(8,128)S(1)} %bitcast.3), custom_call_target="tpu_custom_call" | custom-call | bytes 9437184 | tf_op jit(solution)/shard_map/pallas_call | solution.py:649

commit v9 on v8

--- a/solution.py
+++ b/solution.py
@@ -532,7 +532,7 @@
         igrad[at, cols] = v.astype(BF16)
         return 0
 
-    lax.fori_loop(0, 8, part, 0)
+    lax.fori_loop(0, 8, part, 0, unroll=2)
 
     for j in (2, 6):
         f1y_got(yb, zi(j))

time: 104 us -> 103 us (level)
  no operation moved by 1% of the time
where the time goes in v9:
time: 103 us; the launch traced here: 102 us
  Pallas kernels  101 us (98%)
    pallas_call x1, Pallas kernels, on_device(): pl.pallas_call(body, out_shape=(jax.ShapeDtypeStruct((512, 512), BF16), j...  99.2 us
    pallas_call x1, Pallas kernels, on_device(): pl.pallas_call(leave, out_shape=(jax.ShapeDtypeStruct((512, 512), BF16),...  2.22 us

profile of v9, /device:TPU:2, one launch (start us, length us, event | category | flops | bytes accessed | tf_op | source)
XLA Modules:
  0.0 102.1 jit_solution(17199539543364303678)
XLA Ops:
  0.6 99.2 %shard_map.50 = (bf16[512,512]{1,0:T(8,128)(2,1)S(1)}, f32[4,8,128,256]{3,2,1,0:T(8,128)S(1)}) custom-call(bf16[4,8,16,512]{3,2,1,0:T(8,128)(2,1)} %bitcast.5, bf16[512,256]{1,0:T(8,128)(2,1)} %cot.1, bf16[8,512,256]{2,1,0:T(8,128)(2,1)} %bitcast.4), custom_call_target="tpu_custom_call" | custom-call | flops 4294967296 | bytes 16777216 | tf_op jit(solution)/shard_map/pallas_call | solution.py:580
  99.9 2.2 %shard_map.51 = (bf16[512,512]{1,0:T(8,128)(2,1)}, f32[4096,256]{1,0:T(8,128)}) custom-call(bf16[512,512]{1,0:T(8,128)(2,1)S(1)} %get-tuple-element.4.igrad, f32[4096,256]{1,0:T(8,128)S(1)} %bitcast.3), custom_call_target="tpu_custom_call" | custom-call | bytes 9437184 | tf_op jit(solution)/shard_map/pallas_call | solution.py:649
